TPU v7x, 512 devices: a whole 4x4x16 slice. The times are simulated.
512 devices in a mesh: req: 128 (over z, y, core), tp: 4 (over x).
Axes of the slice: x: 4, y: 4, z: 16, core: 2. Of those that a mesh axis runs over, the one named last changes fastest.
Arguments:
- queries: bfloat16 [512, 2048], P('req', 'tp'), may hold values from -8 to 8
- fresh_key_value: bfloat16 [512, 512], P('req', 'tp'), may hold values from -6 to 6
- key_value_page_pool: bfloat16 [8192, 128, 512], P('req', None, 'tp'), may hold values from -6 to 6
- block_owner: int32 [65536, 1], P('req'), may hold values from 0 to 127; in each aligned block of 512 rows (0 to 511, 512 to 1023, ...) at most 8 rows name the same one
- block_page: int32 [65536], P('req'), may hold values from 0 to 63
- lengths: int32 [512], P('req'), may hold values from 1 to 16384, 4194304 in all
- o_weight: bfloat16 [2048, 2048], P('tp'), may hold values from -0.125 to 0.125
- resid_in: bfloat16 [512, 2048], P('req'), may hold values from -0.59765625 to 0.59765625
- norm_gain: bfloat16 [2048], replicated, may hold values from 0.25 to 1.75
Outputs:
- resid_out: bfloat16 [512, 2048], P('req')
- normed: bfloat16 [512, 2048], P('req')
Inputs may be any that keep to these rules, and one draw needn't show every extreme that they name: `block_owner`: among the 512 block entries of the slots of one index of req, no owner is named more than 8 times.
All inputs are finite; a program needn't handle non-finite values. No bound on the sum of `lengths` on one device may be relied on, other than what follows from the above.
Results may differ from a plain program's by a relative error of at most 0.0047.
Values may be sent and summed in bfloat16 or wider, within the bound.
A program may use at most 64 MiB of HBM per device.

v0:
```python
import math

import jax
import jax.numpy as jnp
from jax import lax
from jax.sharding import PartitionSpec as P

HEAD_WIDTH = 64


SCORE_FLOOR = -1e30
HIGH = lax.Precision.HIGHEST


def page_partials(query_items, meta_items, key_value_page_pool):
    leading = query_items.shape[:-1]
    items = math.prod(leading)
    width = query_items.shape[-1]
    page_len = key_value_page_pool.shape[1]
    kv_local = key_value_page_pool.shape[2] // (2 * HEAD_WIDTH)
    query_group_width = width // (kv_local * HEAD_WIDTH)
    head_count = kv_local * query_group_width
    block_size = math.gcd(items, 128)
    flat_query = query_items.reshape(items // block_size, block_size, width)
    flat_meta = meta_items.reshape(items // block_size, block_size, 3)

    def one_block(block_args):
        block_query, block_meta = block_args
        page_contents = key_value_page_pool[block_meta[:, 0]].reshape(
            block_size, page_len, kv_local, 2, HEAD_WIDTH
        )
        keys = page_contents[:, :, :, 0, :]
        values = page_contents[:, :, :, 1, :]
        query_head_rows = block_query.reshape(block_size, kv_local, query_group_width, HEAD_WIDTH)
        scores = jnp.einsum(
            "ikgd,ipkd->ikgp", query_head_rows, keys, preferred_element_type=jnp.float32
        ) * HEAD_WIDTH ** (-0.5)
        keep_mask = (
            jnp.arange(page_len, dtype=jnp.int32)[None, None, None, :]
            < block_meta[:, 1][:, None, None, None]
        )
        block_max = jnp.max(jnp.where(keep_mask, scores, SCORE_FLOOR), axis=-1)
        probs = jnp.where(keep_mask, jnp.exp(scores - block_max[..., None]), jnp.float32(0.0))
        block_sum = jnp.sum(probs, axis=-1)
        block_out = jnp.einsum(
            "ikgp,ipkd->ikgd",
            probs.astype(jnp.bfloat16),
            values,
            preferred_element_type=jnp.float32,
        )
        return (
            block_out.reshape(block_size, head_count * HEAD_WIDTH),
            block_max.reshape(block_size, head_count),
            block_sum.reshape(block_size, head_count),
        )

    results = lax.map(one_block, (flat_query, flat_meta))
    return tuple((piece.reshape(leading + (piece.shape[-1],)) for piece in results))


def combine(block_out, block_max, block_sum, queries, fresh_key_value):
    slots = queries.shape[0]
    kv_local = fresh_key_value.shape[1] // (2 * HEAD_WIDTH)
    query_group_width = queries.shape[1] // (kv_local * HEAD_WIDTH)
    head_count = kv_local * query_group_width
    entries = block_max.shape[1]
    query_head_rows = queries.reshape(slots, kv_local, query_group_width, HEAD_WIDTH)
    own_token_key_value = fresh_key_value.reshape(slots, kv_local, 2, HEAD_WIDTH)
    self_score = jnp.einsum(
        "skgd,skd->skg",
        query_head_rows,
        own_token_key_value[:, :, 0],
        preferred_element_type=jnp.float32,
    ) * HEAD_WIDTH ** (-0.5)
    self_score = self_score.reshape(slots, head_count)
    top_score = jnp.maximum(jnp.max(block_max, axis=1), self_score)
    weights = jnp.exp(block_max - top_score[:, None])
    self_weight = jnp.exp(self_score - top_score)
    self_value = jnp.broadcast_to(
        own_token_key_value[:, :, 1][:, :, None, :].astype(jnp.float32),
        (slots, kv_local, query_group_width, HEAD_WIDTH),
    ).reshape(slots, head_count, HEAD_WIDTH)
    numer = (
        jnp.einsum(
            "sbh,sbhd->shd",
            weights,
            block_out.reshape(slots, entries, head_count, HEAD_WIDTH),
            precision=HIGH,
        )
        + self_weight[..., None] * self_value
    )
    denom = jnp.sum(weights * block_sum, axis=1) + self_weight
    return (numer / denom[..., None]).reshape(slots, head_count * HEAD_WIDTH).astype(jnp.bfloat16)


def body(
    queries,
    fresh_key_value,
    key_value_page_pool,
    block_owner,
    block_page,
    lengths,
    o_weight,
    resid_in,
    norm_gain,
):
    req_count = lax.axis_size("req")
    slots = queries.shape[0]
    blocks = block_page.shape[0]
    max_blocks = blocks // slots
    page_len = key_value_page_pool.shape[1]
    width = queries.shape[1]
    capacity = max(2, 2 * blocks // req_count)
    owners = block_owner[:, 0]
    onehot = (owners[:, None] == jnp.arange(req_count, dtype=jnp.int32)[None, :]).astype(jnp.int32)
    slot_rank = jnp.sum((jnp.cumsum(onehot, axis=0) - 1) * onehot, axis=1)
    buffer_row = owners * capacity + slot_rank
    slot_of = jnp.arange(blocks, dtype=jnp.int32) // max_blocks
    block_of = jnp.arange(blocks, dtype=jnp.int32) % max_blocks
    live_count = jnp.clip(jnp.repeat(lengths, max_blocks) - block_of * page_len, 0, page_len)
    meta_rows = jnp.stack([block_page, live_count, slot_of], axis=1)
    send_meta = (
        jnp.zeros((req_count * capacity, 3), jnp.int32)
        .at[buffer_row]
        .set(meta_rows)
        .reshape(req_count, capacity, 3)
    )
    send_query = (
        jnp.zeros((req_count * capacity, width), jnp.bfloat16)
        .at[buffer_row]
        .set(jnp.repeat(queries, max_blocks, axis=0))
        .reshape(req_count, capacity, width)
    )
    head_count = width // HEAD_WIDTH
    part_out, part_max, part_sum = page_partials(
        lax.all_to_all(send_query, "req", split_axis=0, concat_axis=0, tiled=True),
        lax.all_to_all(send_meta, "req", split_axis=0, concat_axis=0, tiled=True),
        key_value_page_pool,
    )
    back_out = lax.all_to_all(part_out, "req", split_axis=0, concat_axis=0, tiled=True)
    back_max = lax.all_to_all(part_max, "req", split_axis=0, concat_axis=0, tiled=True)
    back_sum = lax.all_to_all(part_sum, "req", split_axis=0, concat_axis=0, tiled=True)
    block_out = back_out.reshape(req_count * capacity, width)[buffer_row].reshape(
        slots, max_blocks, width
    )
    block_max = back_max.reshape(req_count * capacity, head_count)[buffer_row].reshape(
        slots, max_blocks, head_count
    )
    block_sum = back_sum.reshape(req_count * capacity, head_count)[buffer_row].reshape(
        slots, max_blocks, head_count
    )
    attention = combine(block_out, block_max, block_sum, queries, fresh_key_value)
    gain_f32 = norm_gain.astype(jnp.float32)
    projected = jnp.dot(attention, o_weight, preferred_element_type=jnp.float32)
    stream = resid_in.astype(jnp.float32) + lax.psum(projected, "tp")
    mean_square = jnp.mean(stream * stream, axis=-1, keepdims=True)
    normed = stream * lax.rsqrt(mean_square + 1e-05) * gain_f32
    return (stream.astype(jnp.bfloat16), normed.astype(jnp.bfloat16))


def solution(mesh):
    placed = (
        P("req", "tp"),
        P("req", "tp"),
        P("req", None, "tp"),
        P("req", None),
        P("req"),
        P("req"),
        P("tp", None),
        P("req", None),
        P(),
    )
    return jax.shard_map(
        body,
        mesh=mesh,
        in_specs=placed,
        out_specs=(P("req", None), P("req", None)),
        check_vma=False,
    )
```

profile of v0, /device:TPU:1, one launch (start us, length us, event | category | flops | bytes accessed | tf_op | source)
XLA Modules:
  0.0 478.4 jit_solution(9895010484612518024)
XLA Ops:
  5.1 1.8 scatter_custom_fusion
  8.5 20.6 %all-to-all-start = ((s32[128,8,3]{1,2,0:T(4,128)}), s32[128,8,3]{1,2,0:T(4,128)S(1)}, u32[]{:S(2)}, u32[]{:S(2)}) async-start(s32[128,8,3]{1,2,0:T(4,128)} %copy.52), calls=%async_computation | async-start | bytes 524288 | tf_op jit(solution)/shard_map/all_to_all | solution.py:137
  29.2 3.5 scatter_custom_fusion.1
  32.6 16.9 %all-to-all-done = s32[128,8,3]{1,2,0:T(4,128)S(1)} async-done(((s32[128,8,3]{1,2,0:T(4,128)}), s32[128,8,3]{1,2,0:T(4,128)S(1)}, u32[]{:S(2)}, u32[]{:S(2)}) %all-to-all-start) | async-done | bytes 12320 | tf_op jit(solution)/shard_map/all_to_all | solution.py:137
  49.6 8.8 %all-to-all-start.1 = ((bf16[128,8,512]{2,1,0:T(8,128)(2,1)}), bf16[128,8,512]{2,1,0:T(8,128)(2,1)}, u32[]{:S(2)}, u32[]{:S(2)}) async-start(bf16[128,8,512]{2,1,0:T(8,128)(2,1)} %bitcast.21), calls=%async_computation.1 | async-start | bytes 2097152 | tf_op jit(solution)/shard_map/all_to_all | solution.py:136
  58.5 51.3 %all-to-all-done.1 = bf16[128,8,512]{2,1,0:T(8,128)(2,1)} async-done(((bf16[128,8,512]{2,1,0:T(8,128)(2,1)}), bf16[128,8,512]{2,1,0:T(8,128)(2,1)}, u32[]{:S(2)}, u32[]{:S(2)}) %all-to-all-start.1) | async-done | bytes 1048608 | tf_op jit(solution)/shard_map/all_to_all | solution.py:136
  109.8 157.8 %while.14 = (s32[]{:T(128)}, f32[8,128,512]{2,1,0:T(8,128)}, f32[8,128,8]{2,1,0:T(8,128)}, f32[8,128,8]{2,1,0:T(8,128)S(1)}, s32[8,128,3]{1,0,2:T(8,128)S(1)}, /...) while((s32[]{:T(128)}, f32[8,128,512]{2,1,0:T(8,128)}, f32[8,128,8]{2,1,0:T(8,128)}, ...), condition=%wide.region_8.9_spmd, body=%wide.region_5.8_spmd.sunk | while | flops 34749824 | bytes 25655900 | solution.py:57
  109.9 4.6 gather_fusion
  114.5 6.4 %copy.95 = bf16[128,128,128]{1,2,0:T(8,128)(2,1)} copy(bf16[128,128,128]{2,1,0:T(8,128)(2,1)} %gather_fusion) | data formatting | bytes 8388608 | tf_op jit(solution)/shard_map/while/body/eval_jaxpr/gather | solution.py:29
  122.2 2.3 select_reduce_fusion.2
  125.6 2.8 fusion.42
  129.6 4.6 gather_fusion
  134.2 6.4 %copy.95 = bf16[128,128,128]{1,2,0:T(8,128)(2,1)} copy(bf16[128,128,128]{2,1,0:T(8,128)(2,1)} %gather_fusion) | data formatting | bytes 8388608 | tf_op jit(solution)/shard_map/while/body/eval_jaxpr/gather | solution.py:29
  142.0 2.3 select_reduce_fusion.2
  145.3 2.8 fusion.42
  149.3 4.6 gather_fusion
  154.0 6.4 %copy.95 = bf16[128,128,128]{1,2,0:T(8,128)(2,1)} copy(bf16[128,128,128]{2,1,0:T(8,128)(2,1)} %gather_fusion) | data formatting | bytes 8388608 | tf_op jit(solution)/shard_map/while/body/eval_jaxpr/gather | solution.py:29
  161.7 2.3 select_reduce_fusion.2
  165.0 2.8 fusion.42
  169.0 4.6 gather_fusion
  173.7 6.4 %copy.95 = bf16[128,128,128]{1,2,0:T(8,128)(2,1)} copy(bf16[128,128,128]{2,1,0:T(8,128)(2,1)} %gather_fusion) | data formatting | bytes 8388608 | tf_op jit(solution)/shard_map/while/body/eval_jaxpr/gather | solution.py:29
  181.4 2.3 select_reduce_fusion.2
  184.8 2.8 fusion.42
  188.8 4.6 gather_fusion
  193.4 6.4 %copy.95 = bf16[128,128,128]{1,2,0:T(8,128)(2,1)} copy(bf16[128,128,128]{2,1,0:T(8,128)(2,1)} %gather_fusion) | data formatting | bytes 8388608 | tf_op jit(solution)/shard_map/while/body/eval_jaxpr/gather | solution.py:29
  201.1 2.3 select_reduce_fusion.2
  204.5 2.8 fusion.42
  208.5 4.6 gather_fusion
  213.1 6.4 %copy.95 = bf16[128,128,128]{1,2,0:T(8,128)(2,1)} copy(bf16[128,128,128]{2,1,0:T(8,128)(2,1)} %gather_fusion) | data formatting | bytes 8388608 | tf_op jit(solution)/shard_map/while/body/eval_jaxpr/gather | solution.py:29
  220.8 2.3 select_reduce_fusion.2
  224.2 2.8 fusion.42
  228.2 4.6 gather_fusion
  232.8 6.4 %copy.95 = bf16[128,128,128]{1,2,0:T(8,128)(2,1)} copy(bf16[128,128,128]{2,1,0:T(8,128)(2,1)} %gather_fusion) | data formatting | bytes 8388608 | tf_op jit(solution)/shard_map/while/body/eval_jaxpr/gather | solution.py:29
  240.6 2.3 select_reduce_fusion.2
  243.9 2.8 fusion.42
  247.9 4.6 gather_fusion
  252.6 6.4 %copy.95 = bf16[128,128,128]{1,2,0:T(8,128)(2,1)} copy(bf16[128,128,128]{2,1,0:T(8,128)(2,1)} %gather_fusion) | data formatting | bytes 8388608 | tf_op jit(solution)/shard_map/while/body/eval_jaxpr/gather | solution.py:29
  260.3 2.3 select_reduce_fusion.2
  263.6 2.8 fusion.42
  267.6 10.2 %all-to-all-start.2 = ((f32[128,8,8]{2,1,0:T(8,128)}), f32[128,8,8]{2,1,0:T(8,128)S(1)}, u32[]{:S(2)}, u32[]{:S(2)}) async-start(f32[128,8,8]{2,1,0:T(8,128)} %bitcast.109), calls=%async_computation.2 | async-start | bytes 1048576 | tf_op jit(solution)/shard_map/all_to_all | solution.py:141
  278.8 29.8 %all-to-all-done.2 = f32[128,8,8]{2,1,0:T(8,128)S(1)} async-done(((f32[128,8,8]{2,1,0:T(8,128)}), f32[128,8,8]{2,1,0:T(8,128)S(1)}, u32[]{:S(2)}, u32[]{:S(2)}) %all-to-all-start.2) | async-done | bytes 32800 | tf_op jit(solution)/shard_map/all_to_all | solution.py:141
  308.6 39.9 %all_to_all.25 = f32[128,8,8]{1,2,0:T(8,128)S(1)} all-to-all(f32[128,8,8]{1,2,0:T(8,128)} %copy.60), channel_id=1, replica_groups=mesh['req'=128,'tp'=4] {'req'}, dimensions={0} | all-to-all | bytes 65536 | tf_op jit(solution)/shard_map/all_to_all | solution.py:142
  348.6 9.7 %all-to-all-start.3 = ((f32[128,8,512]{2,1,0:T(8,128)}), f32[128,8,512]{2,1,0:T(8,128)}, u32[]{:S(2)}, u32[]{:S(2)}) async-start(f32[128,8,512]{2,1,0:T(8,128)} %bitcast.107), calls=%async_computation.3 | async-start | bytes 4194304 | tf_op jit(solution)/shard_map/all_to_all | solution.py:140
  361.1 93.7 %all-to-all-done.3 = f32[128,8,512]{2,1,0:T(8,128)} async-done(((f32[128,8,512]{2,1,0:T(8,128)}), f32[128,8,512]{2,1,0:T(8,128)}, u32[]{:S(2)}, u32[]{:S(2)}) %all-to-all-start.3) | async-done | bytes 2097184 | tf_op jit(solution)/shard_map/all_to_all | solution.py:140
  454.8 3.6 gather_fusion.2
  458.4 1.8 reshape.318
  460.2 3.5 fusion.11
  464.3 13.3 %psum.7 = f32[4,2048]{1,0:T(4,128)S(1)} all-reduce(f32[4,2048]{1,0:T(4,128)S(1)} %fusion.30), channel_id=1, replica_groups=mesh['req'=128,'tp'=4] {'tp'}, use_global_device_ids=true, to_apply=%region_11.12 | all-reduce | flops 8192 | bytes 65536 | tf_op jit(solution)/shard_map/psum | solution.py:155
  (156 shorter events, 39.0 us)
Async XLA Ops:
  0.6 463.3 %copy-start = (bf16[512,2048]{1,0:T(8,128)(2,1)S(1)}, bf16[512,2048]{1,0:T(8,128)(2,1)}, u32[]{:S(2)}) copy-start(bf16[512,2048]{1,0:T(8,128)(2,1)} %param.17) | copy-start | bytes 6291460
  0.6 28.5 %copy-start.2 = (bf16[4,512]{1,0:T(4,128)(2,1)S(1)}, bf16[4,512]{1,0:T(4,128)(2,1)}, u32[]{:S(2)}) copy-start(bf16[4,512]{1,0:T(4,128)(2,1)} %param.11) | copy-start | bytes 12292
  8.5 41.0 %all-to-all-start = ((s32[128,8,3]{1,2,0:T(4,128)}), s32[128,8,3]{1,2,0:T(4,128)S(1)}, u32[]{:S(2)}, u32[]{:S(2)}) async-start(s32[128,8,3]{1,2,0:T(4,128)} %copy.52), calls=%async_computation | async-start | bytes 524288 | tf_op jit(solution)/shard_map/all_to_all | solution.py:137
  49.6 60.3 %all-to-all-start.1 = ((bf16[128,8,512]{2,1,0:T(8,128)(2,1)}), bf16[128,8,512]{2,1,0:T(8,128)(2,1)}, u32[]{:S(2)}, u32[]{:S(2)}) async-start(bf16[128,8,512]{2,1,0:T(8,128)(2,1)} %bitcast.21), calls=%async_computation.1 | async-start | bytes 2097152 | tf_op jit(solution)/shard_map/all_to_all | solution.py:136
  267.6 41.0 %all-to-all-start.2 = ((f32[128,8,8]{2,1,0:T(8,128)}), f32[128,8,8]{2,1,0:T(8,128)S(1)}, u32[]{:S(2)}, u32[]{:S(2)}) async-start(f32[128,8,8]{2,1,0:T(8,128)} %bitcast.109), calls=%async_computation.2 | async-start | bytes 1048576 | tf_op jit(solution)/shard_map/all_to_all | solution.py:141
  348.6 9.8 %copy-start.4 = (bf16[4,128]{1,0:T(4,128)(2,1)S(1)}, bf16[4,128]{1,0:T(4,128)(2,1)}, u32[]{:S(2)}) copy-start(bf16[4,128]{1,0:T(4,128)(2,1)} %param.12) | copy-start | bytes 3076
  348.6 9.9 %copy-start.3 = (bf16[2048]{0:T(1024)(128)(2,1)S(1)}, bf16[2048]{0:T(1024)(128)(2,1)}, u32[]{:S(2)}) copy-start(bf16[2048]{0:T(1024)(128)(2,1)} %param.19) | copy-start | bytes 12292
  348.6 106.2 %all-to-all-start.3 = ((f32[128,8,512]{2,1,0:T(8,128)}), f32[128,8,512]{2,1,0:T(8,128)}, u32[]{:S(2)}, u32[]{:S(2)}) async-start(f32[128,8,512]{2,1,0:T(8,128)} %bitcast.107), calls=%async_computation.3 | async-start | bytes 4194304 | tf_op jit(solution)/shard_map/all_to_all | solution.py:140
  460.2 17.4 %copy-start.1 = (bf16[4,2048]{1,0:T(4,128)(2,1)S(1)}, bf16[4,2048]{1,0:T(4,128)(2,1)}, u32[]{:S(2)}) copy-start(bf16[4,2048]{1,0:T(4,128)(2,1)} %param.18) | copy-start | bytes 49156
where the time goes:
time: 485 us; the launch traced here: 478 us
  waiting for transfers between devices  192 us (40%)
  local copies, waits for them, and re-layouts  130 us (27%)
  blocking collectives  53.2 us (11%)
  starting transfers between devices  49.3 us (10%)
  matrix products  45.6 us (9%)
  other arithmetic  7.44 us (2%)
    all_to_all x1, waiting for transfers between devices, body(): lax.all_to_all(part_out, 'req', split_axis=0, concat_axis=0, tiled=True)  93.7 us
    gather x16, local copies, waits for them, and re-layouts, one_block(): key_value_page_pool[block_meta[:, 0]]  88.3 us
    all_to_all x1, waiting for transfers between devices, body(): lax.all_to_all(send_query, 'req', split_axis=0, concat_axis=0, tiled=True)  51.3 us
    all_to_all x1, blocking collectives, body(): lax.all_to_all(part_sum, 'req', split_axis=0, concat_axis=0, tiled=True)  39.9 us
    all_to_all x1, waiting for transfers between devices, body(): lax.all_to_all(part_max, 'req', split_axis=0, concat_axis=0, tiled=True)  29.8 us
    dot_general x8, matrix products, one_block(): jnp.einsum('ikgp,ipkd->ikgd', probs.astype(jnp.bfloat16), values, preferr...  22.8 us
    all_to_all x1, starting transfers between devices, body(): lax.all_to_all(send_meta, 'req', split_axis=0, concat_axis=0, tiled=True)  20.6 us
    dot_general x8, matrix products, one_block(): jnp.einsum('ikgd,ipkd->ikgp', query_head_rows, keys, preferred_element_ty...  18.8 us
  transfers between devices with their start and end apart: 4, of which 4 were waited for; matrix products, arithmetic and copies ran while one was open for 2% of the time, Pallas kernels for 0%

commit v1 on v0

v1 whole, which is shorter than its diff:
```python
import functools

import jax
import jax.numpy as jnp
from jax import lax
from jax.experimental import pallas as pl
from jax.experimental.pallas import tpu as pltpu
from jax.sharding import PartitionSpec as P

F32, BF16, I32 = jnp.float32, jnp.bfloat16, jnp.int32
MESH = pl.DeviceIdType.MESH
NEG = -1e30
CAP = 8
CHUNK = 16
SLOTS = 4
PLANE = 8
VM = pltpu.VMEM


def iota(shape, dim):
    return lax.broadcasted_iota(I32, shape, dim)


def dot_nt(a, b):
    return lax.dot_general(a, b, (((1,), (1,)), ((), ())), preferred_element_type=F32)


def dot_nn(a, b):
    return jnp.dot(a, b, preferred_element_type=F32)


def head_pair_rows(q):
    return jnp.concatenate([q[s : s + 1, 128 * h : 128 * h + 128] for s in range(SLOTS) for h in range(4)], axis=0)


def remote(src, dst, send, recv, peer):
    return pltpu.make_async_remote_copy(
        src_ref=src, dst_ref=dst, send_sem=send, recv_sem=recv, device_id=peer, device_id_type=MESH
    )


def dispatch_kernel(
    nz, q_ref, owner_ref, page_ref, len_ref, qall_ref, mall_ref,
    zq, zsend, zm, ysend, qs_z, qr_z, ms_z, mr_z, qs_y, qr_y, ms_y, mr_y,
):
    me = lax.axis_index("req")
    z, yc = me // PLANE, me % PLANE
    zpeers = [(z + k) % nz for k in range(1, nz)]
    ypeers = [(yc + k) % PLANE for k in range(1, PLANE)]
    barrier = pltpu.get_barrier_semaphore()
    for p in zpeers:
        pl.semaphore_signal(barrier, inc=1, device_id={"req": p * PLANE + yc}, device_id_type=MESH)
    for p in ypeers:
        pl.semaphore_signal(barrier, inc=1, device_id={"req": z * PLANE + p}, device_id_type=MESH)

    zq[z] = head_pair_rows(q_ref[...].astype(F32)).astype(BF16)
    rows, lanes = iota((128, 128), 0), iota((128, 128), 1)
    tri = jnp.where(rows <= lanes, 1.0, 0.0).astype(BF16)
    ones = jnp.ones((128, 128), BF16)
    base = jnp.zeros((128, 128), F32)
    table = jnp.zeros((128, 128), F32)
    for s in range(SLOTS):
        live = jnp.clip(len_ref[s] - iota((1, 128), 1) * 128, 0, 128)
        hit = jnp.logical_and(rows == owner_ref[s : s + 1, :], live > 0)
        hot = jnp.where(hit, 1.0, 0.0).astype(BF16)
        rank = jnp.sum(jnp.where(hit, base + dot_nn(hot, tri) - 1.0, 0.0), axis=0, keepdims=True)
        base = base + dot_nn(hot, ones)
        kind = rows // CAP
        val = jnp.where(
            kind == 0, page_ref[s : s + 1, :].astype(F32),
            jnp.where(kind == 1, live.astype(F32), jnp.where(kind == 2, float(s), 0.0)),
        )
        place = jnp.where((rows % CAP).astype(F32) == rank, val, 0.0).astype(BF16)
        table = table + dot_nt(hot, place)
    zsend[...] = table.reshape(nz, PLANE, 128).astype(BF16)
    zm[z] = zsend[z]

    pl.semaphore_wait(barrier, nz - 1 + PLANE - 1)
    copies = []
    for i, p in enumerate(zpeers):
        to = {"req": p * PLANE + yc}
        copies.append(remote(zq.at[z], zq.at[z], qs_z.at[i], qr_z.at[i], to))
        copies.append(remote(zsend.at[p], zm.at[z], ms_z.at[i], mr_z.at[i], to))
    for c in copies:
        c.start()
    for c in copies:
        c.wait()
    got = zm[...].astype(F32)
    for d in range(PLANE):
        ysend[d] = jnp.concatenate([got[i, d : d + 1, :] for i in range(nz)], axis=0).astype(BF16)
    qall_ref[yc] = zq[...]
    mall_ref[yc] = ysend[yc]
    copies = []
    for i, p in enumerate(ypeers):
        to = {"req": z * PLANE + p}
        copies.append(remote(zq, qall_ref.at[yc], qs_y.at[i], qr_y.at[i], to))
        copies.append(remote(ysend.at[p], mall_ref.at[yc], ms_y.at[i], mr_y.at[i], to))
    for c in copies:
        c.start()
    for c in copies:
        c.wait()


def owner_kernel(
    nz, npages, qall_ref, mall_ref, pool_hbm, po_ref, ps_ref,
    pool, qx, o_s, m_s, l_s, lst_v, sig_v, lst, sig, sems,
):
    nsrc = nz * PLANE
    pool_copy = pltpu.make_async_copy(pool_hbm, pool, sems.at[0])
    pool_copy.start()

    meta = mall_ref[...].astype(F32).reshape(nsrc, 128).T
    page, live, slot = meta[0:8], meta[8:16], meta[16:24]
    valid = live > 0.0
    sig_v[...] = jnp.where(valid, slot, -1.0).astype(I32)
    sig_copy = pltpu.make_async_copy(sig_v, sig, sems.at[1])
    sig_copy.start()

    n8 = npages * 8
    eq = jnp.concatenate([jnp.where(jnp.logical_and(valid, page == float(p)), 1.0, 0.0) for p in range(npages)], axis=0)
    eqb = eq.astype(BF16)
    tri = jnp.where(iota((128, 128), 0) <= iota((128, 128), 1), 1.0, 0.0).astype(BF16)
    cum = dot_nn(eqb, tri)
    tot = dot_nn(eqb, jnp.ones((128, 128), BF16)).astype(BF16)
    ra, rb = iota((n8, n8), 0), iota((n8, n8), 1)
    same = ra // 8 == rb // 8
    before = dot_nn(jnp.where(jnp.logical_and(same, rb < ra), 1.0, 0.0).astype(BF16), tot)
    count = dot_nn(jnp.where(same, 1.0, 0.0).astype(BF16), tot)
    chunks = jnp.floor((count + (CHUNK - 1)) * (1.0 / CHUNK))
    first = dot_nn(
        jnp.where(jnp.logical_and(rb % 8 == 0, rb // 8 < ra // 8), 1.0, 0.0).astype(BF16), chunks.astype(BF16)
    )
    total = (first + chunks)[n8 - 1 : n8, :]
    pos = jnp.sum((eq * (first * CHUNK + before + cum - 1.0)).reshape(npages, 8, 128), axis=0)
    chunk = jnp.floor(pos * (1.0 / CHUNK))
    place = pos - chunk * CHUNK

    krow = iota((CHUNK, 128), 0).astype(F32)
    crow = iota((128, 128), 0).astype(F32)
    src = iota((1, 128), 1).astype(F32)
    lists = jnp.zeros((5 * CHUNK, 128), F32)
    for r in range(CAP):
        row = slice(r, r + 1)
        here = jnp.logical_and(krow == place[row], live[row] > 0.0)
        pick = [jnp.where(here, v, 0.0) for v in (src, float(r + 1), live[row], slot[row], page[row])]
        col = jnp.where(crow == chunk[row], 1.0, 0.0)
        lists = lists + dot_nt(jnp.concatenate(pick, axis=0).astype(BF16), col.astype(BF16))
    srcs, ranks = lists[0:CHUNK], lists[CHUNK : 2 * CHUNK]
    lst_v[0:16] = (srcs * SLOTS + lists[3 * CHUNK : 4 * CHUNK]).astype(I32)
    lst_v[16:32] = jnp.where(ranks > 0.0, (ranks - 1.0) * 128.0 + srcs + 1.0, 0.0).astype(I32)
    lst_v[32:48] = lists[2 * CHUNK : 3 * CHUNK].astype(I32)
    lst_v[48:56] = jnp.concatenate(
        [lists[4 * CHUNK : 4 * CHUNK + 1], total, jnp.zeros((6, 128), F32)], axis=0
    ).astype(I32)
    lst_copy = pltpu.make_async_copy(lst_v, lst, sems.at[2])
    lst_copy.start()

    row8, lane8 = iota((8, 128), 0), iota((8, 128), 1)
    low, left = row8 < 4, lane8 < 64
    keep = jnp.where(left, 0.125, 0.0)

    @pl.loop(0, nsrc)
    def _(i):
        q = qall_ref[i // nz, i % nz].astype(F32)
        for t in range(2):
            v = q[8 * t : 8 * t + 8]
            vs = pltpu.roll(v, 4, 0)
            qx[i * SLOTS + 2 * t] = jnp.where(low, v, pltpu.roll(vs, 64, 1)) * keep
            qx[i * SLOTS + 2 * t + 1] = jnp.where(low, vs, pltpu.roll(v, 64, 1)) * keep

    lst_copy.wait()
    sig_copy.wait()
    pool_copy.wait()
    unroll = 2

    @pl.loop(0, (lst[49, 0] + unroll - 1) // unroll)
    def _(step):
        for u in range(unroll):
            c = step * unroll + u
            kv = pool[lst[48, c]]
            q = jnp.concatenate([qx[lst[k, c]] for k in range(CHUNK)], axis=0).astype(BF16)
            scores = dot_nt(q, kv)
            scores = jnp.concatenate(
                [jnp.where(lane8 < lst[32 + k, c], scores[8 * k : 8 * k + 8], NEG) for k in range(CHUNK)], axis=0
            )
            top = jnp.max(scores, axis=1, keepdims=True)
            probs = jnp.exp(scores - top)
            denom = jnp.sum(probs, axis=1, keepdims=True)
            out = dot_nn(probs.astype(BF16), kv)
            for k in range(CHUNK):
                to = lst[16 + k, c]
                o_s[to] = out[8 * k : 8 * k + 8]
                m_s[to] = jnp.broadcast_to(top[8 * k : 8 * k + 8], (8, 128))
                l_s[to] = jnp.broadcast_to(denom[8 * k : 8 * k + 8], (8, 128))

    for d in range(PLANE):

        def one_source(zi, stat):
            i = d * nz + zi
            slots = [jnp.full((8, 128), sig[r, i], I32) for r in range(CAP)]
            ms = [m_s[1 + r * 128 + i] for r in range(CAP)]
            tops = []
            for s in range(SLOTS):
                top = jnp.full((8, 128), NEG, F32)
                for r in range(CAP):
                    top = jnp.maximum(top, jnp.where(slots[r] == s, ms[r], NEG))
                tops.append(top)
            num = [jnp.zeros((8, 128), F32) for _ in range(SLOTS)]
            den = [jnp.zeros((8, 128), F32) for _ in range(SLOTS)]
            for r in range(CAP):
                top = tops[0]
                for s in range(1, SLOTS):
                    top = jnp.where(slots[r] == s, tops[s], top)
                w = jnp.exp(ms[r] - top)
                o = w * o_s[1 + r * 128 + i]
                l = w * l_s[1 + r * 128 + i]
                for s in range(SLOTS):
                    num[s] = num[s] + jnp.where(slots[r] == s, o, 0.0)
                    den[s] = den[s] + jnp.where(slots[r] == s, l, 0.0)
            outs = []
            for s in range(SLOTS):
                some = den[s] > 0.0
                safe = jnp.where(some, den[s], 1.0)
                outs.append(num[s] / safe)
                lse = jnp.where(some, tops[s] + jnp.log(safe), NEG)
                stat = jnp.where(lane8 == s * nz + zi, lse, stat)
            packed = []
            for t in range(2):
                a, b = outs[2 * t], outs[2 * t + 1]
                first_slot = jnp.where(left, pltpu.roll(a, 64, 1), pltpu.roll(a, 4, 0))
                second = jnp.where(left, pltpu.roll(pltpu.roll(b, 4, 0), 64, 1), b)
                packed.append(jnp.where(low, first_slot, second))
            po_ref[d, zi] = jnp.concatenate(packed, axis=0).astype(BF16)
            return stat

        ps_ref[d] = lax.fori_loop(0, nz, one_source, jnp.full((8, 128), NEG, F32))


def return_kernel(
    nz, ntp, po_ref, ps_ref, q_ref, fresh_ref, w_hbm, resid_ref, gain_ref, res_out, norm_out,
    ro, rs, wn, acc, o1, s1, ro2, rs2, wv, parts,
    os_y, or_y, ss_y, sr_y, os_z, or_z, ss_z, sr_z, ts, tr, wsem,
):
    me, tp = lax.axis_index("req"), lax.axis_index("tp")
    z, yc = me // PLANE, me % PLANE
    zpeers = [(z + k) % nz for k in range(1, nz)]
    ypeers = [(yc + k) % PLANE for k in range(1, PLANE)]
    tpeers = [(tp + k) % ntp for k in range(1, ntp)]
    barrier = pltpu.get_barrier_semaphore()
    for p in zpeers:
        pl.semaphore_signal(barrier, inc=1, device_id={"req": p * PLANE + yc}, device_id_type=MESH)
    for p in ypeers:
        pl.semaphore_signal(barrier, inc=1, device_id={"req": z * PLANE + p}, device_id_type=MESH)
    for p in tpeers:
        pl.semaphore_signal(barrier, inc=1, device_id={"tp": p}, device_id_type=MESH)
    w_copy = pltpu.make_async_copy(w_hbm, wv, wsem.at[0])
    w_copy.start()
    ro[yc] = po_ref[yc]
    rs[yc] = ps_ref[yc]
    pl.semaphore_wait(barrier, nz - 1 + PLANE - 1 + ntp - 1)

    copies = []
    for i, p in enumerate(ypeers):
        to = {"req": z * PLANE + p}
        copies.append(remote(po_ref.at[p], ro.at[yc], os_y.at[i], or_y.at[i], to))
        copies.append(remote(ps_ref.at[p], rs.at[yc], ss_y.at[i], sr_y.at[i], to))
    for c in copies:
        c.start()

    row8, lane8 = iota((8, 128), 0), iota((8, 128), 1)
    low, left = row8 < 4, lane8 < 64
    q16 = head_pair_rows(q_ref[...].astype(F32))
    fresh = fresh_ref[...].astype(F32)
    self_score, self_value = [], []
    for t in range(2):
        kv = jnp.concatenate([fresh[2 * t : 2 * t + 1]] * 4 + [fresh[2 * t + 1 : 2 * t + 2]] * 4, axis=0)
        other = pltpu.roll(kv, 64, 1)
        prod = q16[8 * t : 8 * t + 8] * jnp.where(left, kv, other)
        ls = jnp.sum(jnp.where(left, prod, 0.0), axis=1, keepdims=True)
        rsum = jnp.sum(jnp.where(left, 0.0, prod), axis=1, keepdims=True)
        self_score.append(jnp.where(left, ls, rsum) * 0.125)
        self_value.append(jnp.where(left, other, kv))

    for c in copies:
        c.wait()

    stats = [rs[p] for p in range(PLANE)]
    top = stats[0]
    for p in range(1, PLANE):
        top = jnp.maximum(top, stats[p])
    ws = [jnp.exp(s - top) for s in stats]
    wsum = ws[0]
    for p in range(1, PLANE):
        wsum = wsum + ws[p]
    for p in range(PLANE):
        wn[p] = ws[p] / wsum
    lse = top + jnp.log(wsum)
    acc[...] = jnp.zeros_like(acc)

    def add_part(p, carry):
        x = wn[p]
        xs = pltpu.roll(x, 4, 0)
        yl = jnp.where(low, x, pltpu.roll(xs, 128 - nz, 1))
        yr = jnp.where(low, xs, pltpu.roll(x, 128 - nz, 1))
        for zi in range(nz):
            part = ro[p, zi].astype(F32)
            for t in range(2):
                li = 2 * t * nz + zi
                w = jnp.where(left, yl[:, li : li + 1], yr[:, li : li + 1])
                acc[zi, 8 * t : 8 * t + 8] = acc[zi, 8 * t : 8 * t + 8] + w * part[8 * t : 8 * t + 8]
        return carry

    lax.fori_loop(0, PLANE, add_part, 0)
    o1[...] = acc[...].astype(BF16)
    by_slot = [pltpu.roll(lse, (128 - nz * s) % 128, 1) if s else lse for s in range(SLOTS)]
    rows = jnp.concatenate(by_slot + [jnp.zeros((96, 128), F32)], axis=0).T
    for zi in range(nz):
        s1[zi] = rows[zi : zi + 1]
    ro2[z] = o1[z]
    rs2[z] = s1[z]
    copies = []
    for i, p in enumerate(zpeers):
        to = {"req": p * PLANE + yc}
        copies.append(remote(o1.at[p], ro2.at[z], os_z.at[i], or_z.at[i], to))
        copies.append(remote(s1.at[p], rs2.at[z], ss_z.at[i], sr_z.at[i], to))
    for c in copies:
        c.start()
    for c in copies:
        c.wait()

    st = jnp.concatenate([rs2[zi] for zi in range(nz)], axis=0)
    top = jnp.max(st, axis=0, keepdims=True)
    cols = jnp.concatenate(
        [jnp.exp(st - top), jnp.broadcast_to(top, (8, 128)), jnp.zeros((120 - nz, 128), F32)], axis=0
    ).T
    att = []
    for t in range(2):
        x0, x1 = cols[16 * t : 16 * t + 8], cols[16 * t + 8 : 16 * t + 16]
        yl = jnp.where(low, x0, pltpu.roll(x1, 4, 0))
        yr = jnp.where(low, pltpu.roll(x0, 4, 0), x1)
        num = jnp.zeros((8, 128), F32)
        den = jnp.zeros((8, 128), F32)
        for zi in range(nz):
            w = jnp.where(left, yl[:, zi : zi + 1], yr[:, zi : zi + 1])
            num = num + w * ro2[zi, 8 * t : 8 * t + 8].astype(F32)
            den = den + w
        topm = jnp.where(left, yl[:, nz : nz + 1], yr[:, nz : nz + 1])
        best = jnp.maximum(topm, self_score[t])
        a, b = jnp.exp(topm - best), jnp.exp(self_score[t] - best)
        att.append((a * num + b * self_value[t]) / (a * den + b))
    att = jnp.concatenate(att, axis=0)
    r16 = iota((16, 128), 0)
    wide = jnp.concatenate([jnp.where(r16 % 4 == h, att, 0.0) for h in range(4)], axis=1).astype(BF16)
    sel = jnp.where(iota((16, 16), 1) // 4 == iota((16, 16), 0), 1.0, 0.0).astype(BF16)
    lhs = dot_nn(sel, wide).astype(BF16)
    w_copy.wait()
    parts[tp] = dot_nn(lhs, wv[...])[0:SLOTS]
    copies = []
    for i, p in enumerate(tpeers):
        copies.append(remote(parts.at[tp], parts.at[tp], ts.at[i], tr.at[i], {"tp": p}))
    for c in copies:
        c.start()
    for c in copies:
        c.wait()
    stream = parts[0]
    for p in range(1, ntp):
        stream = stream + parts[p]
    stream = resid_ref[...].astype(F32) + stream
    mean = jnp.mean(stream * stream, axis=1, keepdims=True)
    res_out[...] = stream.astype(BF16)
    norm_out[...] = (stream * lax.rsqrt(mean + 1e-5) * gain_ref[...].astype(F32)).astype(BF16)


def vmem(n):
    return [pl.BlockSpec(memory_space=pltpu.VMEM)] * n


ANY = pl.BlockSpec(memory_space=pl.ANY)


def body(nz, ntp, queries, fresh_key_value, pool, block_owner, block_page, lengths, o_weight, resid_in, norm_gain):
    npages = pool.shape[0]
    width = o_weight.shape[1]
    DMA = pltpu.SemaphoreType.DMA
    qall, mall = pl.pallas_call(
        functools.partial(dispatch_kernel, nz),
        out_shape=(
            jax.ShapeDtypeStruct((PLANE, nz, 16, 128), BF16),
            jax.ShapeDtypeStruct((PLANE, nz, 128), BF16),
        ),
        in_specs=vmem(3) + [pl.BlockSpec(memory_space=pltpu.SMEM)],
        out_specs=tuple(vmem(2)),
        scratch_shapes=[
            VM((nz, 16, 128), BF16), VM((nz, PLANE, 128), BF16), VM((nz, PLANE, 128), BF16),
            VM((PLANE, nz, 128), BF16),
        ]
        + [DMA((nz - 1,))] * 4 + [DMA((PLANE - 1,))] * 4,
        compiler_params=pltpu.CompilerParams(collective_id=0, has_side_effects=True),
        name="dispatch",
    )(queries, block_owner.reshape(SLOTS, 128), block_page.reshape(SLOTS, 128), lengths)

    po, ps = pl.pallas_call(
        functools.partial(owner_kernel, nz, npages),
        out_shape=(
            jax.ShapeDtypeStruct((PLANE, nz, 16, 128), BF16),
            jax.ShapeDtypeStruct((PLANE, 8, 128), F32),
        ),
        in_specs=vmem(2) + [ANY],
        out_specs=tuple(vmem(2)),
        scratch_shapes=[
            VM(pool.shape, BF16),
            VM((PLANE * nz * SLOTS, 8, 128), F32),
            VM((1032, 8, 128), F32), VM((1032, 8, 128), F32), VM((1032, 8, 128), F32),
            VM((56, 128), I32), VM((8, 128), I32),
            pltpu.SMEM((56, 128), I32), pltpu.SMEM((8, 128), I32),
            DMA((3,)),
        ],
        compiler_params=pltpu.CompilerParams(vmem_limit_bytes=40 << 20),
        name="owner",
    )(qall, mall, pool)

    return pl.pallas_call(
        functools.partial(return_kernel, nz, ntp),
        out_shape=(
            jax.ShapeDtypeStruct((SLOTS, width), BF16),
            jax.ShapeDtypeStruct((SLOTS, width), BF16),
        ),
        in_specs=vmem(4) + [ANY] + vmem(2),
        out_specs=tuple(vmem(2)),
        scratch_shapes=[
            VM((PLANE, nz, 16, 128), BF16), VM((PLANE, 8, 128), F32), VM((PLANE, 8, 128), F32),
            VM((nz, 16, 128), F32), VM((nz, 16, 128), BF16), VM((nz, 1, 128), F32),
            VM((nz, 16, 128), BF16), VM((nz, 1, 128), F32), VM(o_weight.shape, BF16),
            VM((ntp, SLOTS, width), F32),
        ]
        + [DMA((PLANE - 1,))] * 4 + [DMA((nz - 1,))] * 4 + [DMA((ntp - 1,))] * 2 + [DMA((1,))],
        compiler_params=pltpu.CompilerParams(
            collective_id=1, has_side_effects=True, vmem_limit_bytes=24 << 20
        ),
        name="give_back",
    )(po, ps, queries, fresh_key_value, o_weight, resid_in, norm_gain.reshape(1, width))


def solution(mesh):
    nz, ntp = mesh.shape["req"] // PLANE, mesh.shape["tp"]
    placed = (
        P("req", "tp"), P("req", "tp"), P("req", None, "tp"), P("req", None), P("req"), P("req"),
        P("tp", None), P("req", None), P(),
    )
    return jax.shard_map(
        functools.partial(body, nz, ntp),
        mesh=mesh,
        in_specs=placed,
        out_specs=(P("req", None), P("req", None)),
        check_vma=False,
    )
```

time: 485 us -> 117 us (0.24); the launches traced: 478 us -> 116 us
  waiting for transfers between devices: 192 us -> 0 us
  local copies, waits for them, and re-layouts: 130 us -> 4.62 us
  Pallas kernels: 0 us -> 111 us
  blocking collectives: 53.2 us -> 0 us
  starting transfers between devices: 49.3 us -> 0 us
  matrix products: 45.6 us -> 0 us
  other arithmetic: 7.44 us -> 0 us
    all_to_all x4 -> x0, waiting for transfers between devices: 192 us -> none  [the longest x1 93.7 us: body(): lax.all_to_all(part_out, 'req', split_axis=0, concat_axis=0, tiled=True)]
    pallas_call x0 -> x3, Pallas kernels: none -> 111 us  [the longest x1 45.7 us: body(): pl.pallas_call(functools.partial(owner_kernel, nz, npages), out_shape=(ja...]
    gather x19 -> x0, local copies, waits for them, and re-layouts: 94 us -> none  [the longest x16 88.3 us: one_block(): key_value_page_pool[block_meta[:, 0]]]
    all_to_all x4 -> x0, starting transfers between devices: 49.3 us -> none  [the longest x1 20.6 us: body(): lax.all_to_all(send_meta, 'req', split_axis=0, concat_axis=0, tiled=True)]
    dot_general x19 -> x0, matrix products: 45.6 us -> none  [the longest x8 22.8 us: one_block(): jnp.einsum('ikgp,ipkd->ikgd', probs.astype(jnp.bfloat16), values, preferr...]
    all_to_all x1 -> x0, blocking collectives: 39.9 us -> none  [body(): lax.all_to_all(part_sum, 'req', split_axis=0, concat_axis=0, tiled=True)]
    psum x1 -> x0, blocking collectives: 13.3 us -> none  [body(): stream = resid_in.astype(jnp.float32) + lax.psum(projected, 'tp')]
    dynamic_update_slice x24 -> x0, local copies, waits for them, and re-layouts: 12.1 us -> none  [page_partials(): results = lax.map(one_block, (flat_query, flat_meta))]
  transfers between devices with their start and end apart: 4 -> 0, of which waited for: 4 -> 0; matrix products, arithmetic and copies ran while one was open for 2% -> 0% of each run, Pallas kernels for 0% -> 0%
where the time goes in v1:
time: 117 us; the launch traced here: 116 us
  Pallas kernels  111 us (95%)
  local copies, waits for them, and re-layouts  4.62 us (4%)
    pallas_call x1, Pallas kernels, body(): pl.pallas_call(functools.partial(owner_kernel, nz, npages), out_shape=(ja...  45.7 us
    pallas_call x1, Pallas kernels, body(): pl.pallas_call(functools.partial(dispatch_kernel, nz), out_shape=(jax.Sha...  33.3 us
    pallas_call x1, Pallas kernels, body(): pl.pallas_call(functools.partial(return_kernel, nz, ntp), out_shape=(jax....  32.1 us
    unnamed x18, local copies, waits for them, and re-layouts  4.62 us

profile of v1, /device:TPU:1, one launch (start us, length us, event | category | flops | bytes accessed | tf_op | source)
XLA Modules:
  0.0 116.4 jit_solution(14360491563557702850)
XLA Ops:
  0.6 0.0 copy-start
  0.6 33.3 %dispatch.1 = (bf16[8,16,16,128]{3,2,1,0:T(8,128)(2,1)}, bf16[8,16,128]{2,1,0:T(8,128)(2,1)}) custom-call(bf16[4,512]{1,0:T(4,128)(2,1)} %q_ref.3, s32[4,128]{1,0:T(4,128)} %bitcast.2, s32[4,128]{1,0:T(4,128)} %bitcast.3, s32[4]{0:T(128)} %len_ref.1), custom_call_target="tpu_custom_call" | custom-call | tf_op jit(solution)/shard_map/dispatch/pallas_call | solution.py:385
  33.9 0.0 copy-start.1
  33.9 1.6 %copy-done.1 = bf16[64,128,128]{2,1,0:T(8,128)(2,1)S(1)} copy-done((bf16[64,128,128]{2,1,0:T(8,128)(2,1)S(1)}, bf16[64,128,128]{2,1,0:T(8,128)(2,1)}, u32[]{:S(2)}) %copy-start.1) | copy-done | bytes 2097176
  35.5 0.0 copy-start.2
  35.5 1.0 copy-done.2
  36.5 0.0 copy-start.3
  36.5 0.8 copy-done.3
  37.3 0.0 copy-start.7
  37.3 0.0 copy-start.4
  37.3 0.0 copy-start.5
  37.3 0.0 copy-start.6
  37.3 45.7 %owner.1 = (bf16[8,16,16,128]{3,2,1,0:T(8,128)(2,1)S(1)}, f32[8,8,128]{2,1,0:T(8,128)S(1)}) custom-call(bf16[8,16,16,128]{3,2,1,0:T(8,128)(2,1)S(1)} %copy-done.2, bf16[8,16,128]{2,1,0:T(8,128)(2,1)S(1)} %copy-done.3, bf16[64,128,128]{2,1,0:T(8,128)(2,1)S(1)} %copy-done.1), custom_call_target="tpu_custom_call" | custom-call | tf_op jit(solution)/shard_map/owner/pallas_call | solution.py:402
  83.0 0.0 copy-done.7
  83.0 0.0 copy-done
  83.1 0.0 copy-done.4
  83.1 0.0 copy-done.5
  83.1 0.0 copy-done.6
  83.1 32.1 %give_back.1 = (bf16[4,2048]{1,0:T(4,128)(2,1)S(1)}, bf16[4,2048]{1,0:T(4,128)(2,1)S(1)}) custom-call(bf16[8,16,16,128]{3,2,1,0:T(8,128)(2,1)S(1)} %get-tuple-element.8.po_ref, f32[8,8,128]{2,1,0:T(8,128)S(1)} %get-tuple-element.9.ps_ref, bf16[4,512]{1,0:T(4,128)(2,1)S(1)} %copy-done.5, bf16[4,128]{1,0:T(4,128)(2,1)S(1)} %copy-done.6, ...), custom_call_target="tpu_custom_call" | custom-call | tf_op jit(solution)/shard_map/give_back/pallas_call | solution.py:422
  115.1 0.6 copy.13
  115.8 0.6 copy.14
  (1 shorter events, 0.0 us)
Async XLA Ops:
  0.6 82.4 %copy-start = (bf16[512,2048]{1,0:T(8,128)(2,1)S(1)}, bf16[512,2048]{1,0:T(8,128)(2,1)}, u32[]{:S(2)}) copy-start(bf16[512,2048]{1,0:T(8,128)(2,1)} %w_hbm.1) | copy-start | bytes 6291460
  33.9 1.6 %copy-start.1 = (bf16[64,128,128]{2,1,0:T(8,128)(2,1)S(1)}, bf16[64,128,128]{2,1,0:T(8,128)(2,1)}, u32[]{:S(2)}) copy-start(bf16[64,128,128]{2,1,0:T(8,128)(2,1)} %pool_hbm.1) | copy-start | bytes 6291460
  35.5 1.0 copy-start.2
  36.5 0.8 copy-start.3
  37.3 45.7 %copy-start.7 = (bf16[2048]{0:T(1024)(128)(2,1)S(1)}, bf16[2048]{0:T(1024)(128)(2,1)}, u32[]{:S(2)}) copy-start(bf16[2048]{0:T(1024)(128)(2,1)} %param.17) | copy-start | bytes 12292
  37.3 45.7 %copy-start.4 = (bf16[4,2048]{1,0:T(4,128)(2,1)S(1)}, bf16[4,2048]{1,0:T(4,128)(2,1)}, u32[]{:S(2)}) copy-start(bf16[4,2048]{1,0:T(4,128)(2,1)} %resid_ref.1) | copy-start | bytes 49156
  37.3 45.8 %copy-start.5 = (bf16[4,512]{1,0:T(4,128)(2,1)S(1)}, bf16[4,512]{1,0:T(4,128)(2,1)}, u32[]{:S(2)}) copy-start(bf16[4,512]{1,0:T(4,128)(2,1)} %q_ref.3) | copy-start | bytes 12292
  37.3 45.8 %copy-start.6 = (bf16[4,128]{1,0:T(4,128)(2,1)S(1)}, bf16[4,128]{1,0:T(4,128)(2,1)}, u32[]{:S(2)}) copy-start(bf16[4,128]{1,0:T(4,128)(2,1)} %fresh_ref.1) | copy-start | bytes 3076

commit v2 on v1

--- a/solution.py
+++ b/solution.py
@@ -102,38 +102,33 @@
 
 
 def owner_kernel(
-    nz, npages, qall_ref, mall_ref, pool_hbm, po_ref, ps_ref,
-    pool, qx, o_s, m_s, l_s, lst_v, sig_v, lst, sig, sems,
+    nz, npages, qall_ref, mall_ref, pool, po_ref, ps_ref,
+    qx, o_s, ml_s, wn_s, sg_s, s0, s1, p0, p1, lst_v, lst, sems,
 ):
     nsrc = nz * PLANE
-    pool_copy = pltpu.make_async_copy(pool_hbm, pool, sems.at[0])
-    pool_copy.start()
-
-    meta = mall_ref[...].astype(F32).reshape(nsrc, 128).T
+    row8, lane8 = iota((8, 128), 0), iota((8, 128), 1)
+    low, left = row8 < 4, lane8 < 64
+    meta_b = mall_ref[...].reshape(nsrc, 128)
+    meta = meta_b.astype(F32).T
     page, live, slot = meta[0:8], meta[8:16], meta[16:24]
     valid = live > 0.0
-    sig_v[...] = jnp.where(valid, slot, -1.0).astype(I32)
-    sig_copy = pltpu.make_async_copy(sig_v, sig, sems.at[1])
-    sig_copy.start()
-
-    n8 = npages * 8
-    eq = jnp.concatenate([jnp.where(jnp.logical_and(valid, page == float(p)), 1.0, 0.0) for p in range(npages)], axis=0)
-    eqb = eq.astype(BF16)
-    tri = jnp.where(iota((128, 128), 0) <= iota((128, 128), 1), 1.0, 0.0).astype(BF16)
-    cum = dot_nn(eqb, tri)
-    tot = dot_nn(eqb, jnp.ones((128, 128), BF16)).astype(BF16)
-    ra, rb = iota((n8, n8), 0), iota((n8, n8), 1)
-    same = ra // 8 == rb // 8
-    before = dot_nn(jnp.where(jnp.logical_and(same, rb < ra), 1.0, 0.0).astype(BF16), tot)
-    count = dot_nn(jnp.where(same, 1.0, 0.0).astype(BF16), tot)
-    chunks = jnp.floor((count + (CHUNK - 1)) * (1.0 / CHUNK))
-    first = dot_nn(
-        jnp.where(jnp.logical_and(rb % 8 == 0, rb // 8 < ra // 8), 1.0, 0.0).astype(BF16), chunks.astype(BF16)
-    )
-    total = (first + chunks)[n8 - 1 : n8, :]
-    pos = jnp.sum((eq * (first * CHUNK + before + cum - 1.0)).reshape(npages, 8, 128), axis=0)
-    chunk = jnp.floor(pos * (1.0 / CHUNK))
-    place = pos - chunk * CHUNK
+
+    prow = iota((npages, 128), 0).astype(F32)
+    eqs = [
+        jnp.where(jnp.logical_and(prow == page[r : r + 1], live[r : r + 1] > 0.0), 1.0, 0.0) for r in range(CAP)
+    ]
+    upto = jnp.where(iota((128, 256), 0) <= iota((128, 256), 1), 1.0, 0.0).astype(BF16)
+    counts = dot_nn(jnp.concatenate(eqs, axis=0).astype(BF16), upto)
+    run = jnp.zeros((npages, 128), F32)
+    ranks = []
+    for r in range(CAP):
+        part = counts[npages * r : npages * r + npages]
+        ranks.append(run + part[:, 0:128])
+        run = run + part[:, 128:256]
+    chunks = jnp.floor((run + (CHUNK - 1)) * (1.0 / CHUNK))
+    below = jnp.where(iota((npages, npages), 1) < iota((npages, npages), 0), 1.0, 0.0).astype(BF16)
+    first = dot_nn(below, chunks.astype(BF16))
+    total = (first + chunks)[npages - 1 : npages]
 
     krow = iota((CHUNK, 128), 0).astype(F32)
     crow = iota((128, 128), 0).astype(F32)
@@ -141,99 +136,146 @@
     lists = jnp.zeros((5 * CHUNK, 128), F32)
     for r in range(CAP):
         row = slice(r, r + 1)
-        here = jnp.logical_and(krow == place[row], live[row] > 0.0)
+        pos = jnp.sum(eqs[r] * (first * CHUNK + ranks[r] - 1.0), axis=0, keepdims=True)
+        chunk = jnp.floor(pos * (1.0 / CHUNK))
+        here = jnp.logical_and(krow == pos - chunk * CHUNK, live[row] > 0.0)
         pick = [jnp.where(here, v, 0.0) for v in (src, float(r + 1), live[row], slot[row], page[row])]
-        col = jnp.where(crow == chunk[row], 1.0, 0.0)
+        col = jnp.where(crow == chunk, 1.0, 0.0)
         lists = lists + dot_nt(jnp.concatenate(pick, axis=0).astype(BF16), col.astype(BF16))
-    srcs, ranks = lists[0:CHUNK], lists[CHUNK : 2 * CHUNK]
+    srcs, nth = lists[0:CHUNK], lists[CHUNK : 2 * CHUNK]
     lst_v[0:16] = (srcs * SLOTS + lists[3 * CHUNK : 4 * CHUNK]).astype(I32)
-    lst_v[16:32] = jnp.where(ranks > 0.0, (ranks - 1.0) * 128.0 + srcs + 1.0, 0.0).astype(I32)
+    lst_v[16:32] = jnp.where(nth > 0.0, srcs * CAP + nth - 1.0, float(nsrc * CAP)).astype(I32)
     lst_v[32:48] = lists[2 * CHUNK : 3 * CHUNK].astype(I32)
     lst_v[48:56] = jnp.concatenate(
         [lists[4 * CHUNK : 4 * CHUNK + 1], total, jnp.zeros((6, 128), F32)], axis=0
     ).astype(I32)
-    lst_copy = pltpu.make_async_copy(lst_v, lst, sems.at[2])
+    lst_copy = pltpu.make_async_copy(lst_v, lst, sems.at[0])
     lst_copy.start()
 
-    row8, lane8 = iota((8, 128), 0), iota((8, 128), 1)
-    low, left = row8 < 4, lane8 < 64
     keep = jnp.where(left, 0.125, 0.0)
-
-    @pl.loop(0, nsrc)
-    def _(i):
-        q = qall_ref[i // nz, i % nz].astype(F32)
-        for t in range(2):
-            v = q[8 * t : 8 * t + 8]
-            vs = pltpu.roll(v, 4, 0)
-            qx[i * SLOTS + 2 * t] = jnp.where(low, v, pltpu.roll(vs, 64, 1)) * keep
-            qx[i * SLOTS + 2 * t + 1] = jnp.where(low, vs, pltpu.roll(v, 64, 1)) * keep
-
+    group = 8
+
+    @pl.loop(0, nsrc // group)
+    def _(g):
+        for u in range(group):
+            i = g * group + u
+            q = qall_ref[i // nz, i % nz].astype(F32)
+            for t in range(2):
+                v = q[8 * t : 8 * t + 8]
+                vs = pltpu.roll(v, 4, 0)
+                qx[i * SLOTS + 2 * t] = jnp.where(low, v, pltpu.roll(vs, 64, 1)) * keep
+                qx[i * SLOTS + 2 * t + 1] = jnp.where(low, vs, pltpu.roll(v, 64, 1)) * keep
+
+    spread = jnp.where(iota((128, 128), 0) == 2 * CAP + iota((128, 128), 1) // 8 % CAP, 1.0, 0.0).astype(BF16)
+    sg_s[...] = dot_nn(meta_b, spread)
     lst_copy.wait()
-    sig_copy.wait()
-    pool_copy.wait()
-    unroll = 2
-
-    @pl.loop(0, (lst[49, 0] + unroll - 1) // unroll)
+
+    def scores_of(c, out):
+        c = jnp.clip(c, 0, 127)
+        q = jnp.concatenate([qx[lst[k, c]] for k in range(CHUNK)], axis=0).astype(BF16)
+        out[...] = dot_nt(q, pool[lst[48, c]])
+
+    def probs_of(c, scores, out):
+        c = jnp.clip(c, 0, 127)
+        pair = []
+        for k in range(CHUNK):
+            sc = jnp.where(lane8 < lst[32 + k, c], scores[8 * k : 8 * k + 8], NEG)
+            top = jnp.max(sc, axis=1, keepdims=True)
+            pr = jnp.exp(sc - top)
+            ml_s[lst[16 + k, c]] = jnp.where(left, top, jnp.sum(pr, axis=1, keepdims=True))
+            pair.append(pr)
+            if k % 2:
+                out[8 * k - 8 : 8 * k + 8] = jnp.concatenate(pair, axis=0).astype(BF16)
+                pair = []
+
+    def values_of(c, probs):
+        c = jnp.clip(c, 0, 127)
+        out = dot_nn(probs[...], pool[lst[48, c]])
+        for k in range(CHUNK):
+            o_s[lst[16 + k, c]] = out[8 * k : 8 * k + 8]
+
+    @pl.loop(0, (lst[49, 0] + 3) // 2)
     def _(step):
-        for u in range(unroll):
-            c = step * unroll + u
-            kv = pool[lst[48, c]]
-            q = jnp.concatenate([qx[lst[k, c]] for k in range(CHUNK)], axis=0).astype(BF16)
-            scores = dot_nt(q, kv)
-            scores = jnp.concatenate(
-                [jnp.where(lane8 < lst[32 + k, c], scores[8 * k : 8 * k + 8], NEG) for k in range(CHUNK)], axis=0
-            )
-            top = jnp.max(scores, axis=1, keepdims=True)
-            probs = jnp.exp(scores - top)
-            denom = jnp.sum(probs, axis=1, keepdims=True)
-            out = dot_nn(probs.astype(BF16), kv)
-            for k in range(CHUNK):
-                to = lst[16 + k, c]
-                o_s[to] = out[8 * k : 8 * k + 8]
-                m_s[to] = jnp.broadcast_to(top[8 * k : 8 * k + 8], (8, 128))
-                l_s[to] = jnp.broadcast_to(denom[8 * k : 8 * k + 8], (8, 128))
-
+        c = 2 * step
+        scores_of(c, s0)
+        probs_of(c - 1, s1, p1)
+        values_of(c - 2, p0)
+        scores_of(c + 1, s1)
+        probs_of(c, s0, p0)
+        values_of(c - 1, p1)
+
+    halves = []
+    for h in range(2):
+
+        def gather(g, accs, h=h):
+            accs = list(accs)
+            for u in range(8):
+                i = g * 8 + u
+                mask = lane8 % 64 == i
+                for r in range(CAP):
+                    accs[r] = jnp.where(mask, ml_s[(h * 64 + i) * CAP + r], accs[r])
+            return tuple(accs)
+
+        halves.append(lax.fori_loop(0, 8, gather, tuple(jnp.zeros((8, 128), F32) for _ in range(CAP))))
+    mine = [[jnp.logical_and(live[r : r + 1] > 0.0, slot[r : r + 1] == float(s)) for s in range(SLOTS)] for r in range(CAP)]
+    ms = [jnp.where(left, halves[0][r], pltpu.roll(halves[1][r], 64, 1)) for r in range(CAP)]
+    ls = [jnp.where(left, pltpu.roll(halves[0][r], 64, 1), halves[1][r]) for r in range(CAP)]
+    tops, dens = [], []
+    for s in range(SLOTS):
+        top = jnp.full((8, 128), NEG, F32)
+        for r in range(CAP):
+            top = jnp.maximum(top, jnp.where(mine[r][s], ms[r], NEG))
+        tops.append(top)
+    es = []
+    for r in range(CAP):
+        top = ms[r]
+        for s in range(SLOTS):
+            top = jnp.where(mine[r][s], tops[s], top)
+        es.append(jnp.exp(ms[r] - top))
+    lses, invs = [], []
+    for s in range(SLOTS):
+        den = jnp.zeros((8, 128), F32)
+        for r in range(CAP):
+            den = den + jnp.where(mine[r][s], es[r] * ls[r], 0.0)
+        some = den > 0.0
+        den = jnp.where(some, den, 1.0)
+        invs.append(1.0 / den)
+        lses.append(jnp.where(some, tops[s] + jnp.log(den), NEG))
+    for r in range(CAP):
+        w = jnp.zeros((8, 128), F32)
+        for s in range(SLOTS):
+            w = jnp.where(mine[r][s], es[r] * invs[s], w)
+        wn_s[r] = w
     for d in range(PLANE):
-
-        def one_source(zi, stat):
-            i = d * nz + zi
-            slots = [jnp.full((8, 128), sig[r, i], I32) for r in range(CAP)]
-            ms = [m_s[1 + r * 128 + i] for r in range(CAP)]
-            tops = []
-            for s in range(SLOTS):
-                top = jnp.full((8, 128), NEG, F32)
+        stat = jnp.full((8, 128), NEG, F32)
+        for s in range(SLOTS):
+            shift = (nz * (s - d)) % 128
+            moved = pltpu.roll(lses[s], shift, 1) if shift else lses[s]
+            stat = jnp.where(lane8 // nz == s, moved, stat)
+        ps_ref[d] = stat
+
+    ar, al = iota((64, 128), 0), iota((64, 128), 1)
+    same = jnp.logical_and(ar // 32 == al // 64, ar // 16 % 2 * 4 + ar % 4 == al % 8)
+    want = jnp.where(same, ar // 4 % 4, -1).astype(F32)
+    left16 = iota((16, 128), 1) < 64
+
+    @pl.loop(0, PLANE)
+    def _(d):
+        ws = [pltpu.roll(wn_s[r], (128 - nz * d) % 128, 1) for r in range(CAP)]
+        for j in range(nz // 2):
+            scaled = []
+            for a in range(2):
                 for r in range(CAP):
-                    top = jnp.maximum(top, jnp.where(slots[r] == s, ms[r], NEG))
-                tops.append(top)
-            num = [jnp.zeros((8, 128), F32) for _ in range(SLOTS)]
-            den = [jnp.zeros((8, 128), F32) for _ in range(SLOTS)]
-            for r in range(CAP):
-                top = tops[0]
-                for s in range(1, SLOTS):
-                    top = jnp.where(slots[r] == s, tops[s], top)
-                w = jnp.exp(ms[r] - top)
-                o = w * o_s[1 + r * 128 + i]
-                l = w * l_s[1 + r * 128 + i]
-                for s in range(SLOTS):
-                    num[s] = num[s] + jnp.where(slots[r] == s, o, 0.0)
-                    den[s] = den[s] + jnp.where(slots[r] == s, l, 0.0)
-            outs = []
-            for s in range(SLOTS):
-                some = den[s] > 0.0
-                safe = jnp.where(some, den[s], 1.0)
-                outs.append(num[s] / safe)
-                lse = jnp.where(some, tops[s] + jnp.log(safe), NEG)
-                stat = jnp.where(lane8 == s * nz + zi, lse, stat)
-            packed = []
-            for t in range(2):
-                a, b = outs[2 * t], outs[2 * t + 1]
-                first_slot = jnp.where(left, pltpu.roll(a, 64, 1), pltpu.roll(a, 4, 0))
-                second = jnp.where(left, pltpu.roll(pltpu.roll(b, 4, 0), 64, 1), b)
-                packed.append(jnp.where(low, first_slot, second))
-            po_ref[d, zi] = jnp.concatenate(packed, axis=0).astype(BF16)
-            return stat
-
-        ps_ref[d] = lax.fori_loop(0, nz, one_source, jnp.full((8, 128), NEG, F32))
+                    w = jnp.broadcast_to(ws[r][:, 2 * j + a : 2 * j + a + 1], (8, 128))
+                    o = o_s[(d * nz + 2 * j + a) * CAP + r]
+                    scaled.append(jnp.where(w > 0.0, o * w, 0.0))
+            i = d * nz + 2 * j
+            sg = jnp.where(lane8[0:1] < 64, sg_s[pl.ds(i, 1), :], sg_s[pl.ds(i + 1, 1), :])
+            pickm = jnp.where(want == sg, 1.0, 0.0).astype(BF16)
+            res = dot_nn(pickm, jnp.concatenate(scaled, axis=0).astype(BF16))
+            for a in range(2):
+                even, odd = res[32 * a : 32 * a + 16], res[32 * a + 16 : 32 * a + 32]
+                po_ref[d, 2 * j + a] = jnp.where(left16, pltpu.roll(even, 64, 1), odd).astype(BF16)
 
 
 def return_kernel(
@@ -378,8 +420,30 @@
 ANY = pl.BlockSpec(memory_space=pl.ANY)
 
 
+def owner_call(nz, qall, mall, pool):
+    nsrc = nz * PLANE
+    return pl.pallas_call(
+        functools.partial(owner_kernel, nz, pool.shape[0]),
+        out_shape=(
+            jax.ShapeDtypeStruct((PLANE, nz, 16, 128), BF16),
+            jax.ShapeDtypeStruct((PLANE, 8, 128), F32),
+        ),
+        in_specs=vmem(3),
+        out_specs=tuple(vmem(2)),
+        scratch_shapes=[
+            VM((nsrc * SLOTS, 8, 128), F32),
+            VM((nsrc * CAP + 1, 8, 128), F32), VM((nsrc * CAP + 1, 8, 128), F32),
+            VM((CAP, 8, 128), F32), VM((nsrc, 128), F32),
+            VM((128, 128), F32), VM((128, 128), F32), VM((128, 128), BF16), VM((128, 128), BF16),
+            VM((56, 128), I32), pltpu.SMEM((56, 128), I32),
+            pltpu.SemaphoreType.DMA((1,)),
+        ],
+        compiler_params=pltpu.CompilerParams(vmem_limit_bytes=20 << 20),
+        name="owner",
+    )(qall, mall, pool)
+
+
 def body(nz, ntp, queries, fresh_key_value, pool, block_owner, block_page, lengths, o_weight, resid_in, norm_gain):
-    npages = pool.shape[0]
     width = o_weight.shape[1]
     DMA = pltpu.SemaphoreType.DMA
     qall, mall = pl.pallas_call(
@@ -395,30 +459,13 @@
             VM((PLANE, nz, 128), BF16),
         ]
         + [DMA((nz - 1,))] * 4 + [DMA((PLANE - 1,))] * 4,
-        compiler_params=pltpu.CompilerParams(collective_id=0, has_side_effects=True),
+        compiler_params=pltpu.CompilerParams(
+            collective_id=0, has_side_effects=True, vmem_limit_bytes=6 << 20
+        ),
         name="dispatch",
     )(queries, block_owner.reshape(SLOTS, 128), block_page.reshape(SLOTS, 128), lengths)
 
-    po, ps = pl.pallas_call(
-        functools.partial(owner_kernel, nz, npages),
-        out_shape=(
-            jax.ShapeDtypeStruct((PLANE, nz, 16, 128), BF16),
-            jax.ShapeDtypeStruct((PLANE, 8, 128), F32),
-        ),
-        in_specs=vmem(2) + [ANY],
-        out_specs=tuple(vmem(2)),
-        scratch_shapes=[
-            VM(pool.shape, BF16),
-            VM((PLANE * nz * SLOTS, 8, 128), F32),
-            VM((1032, 8, 128), F32), VM((1032, 8, 128), F32), VM((1032, 8, 128), F32),
-            VM((56, 128), I32), VM((8, 128), I32),
-            pltpu.SMEM((56, 128), I32), pltpu.SMEM((8, 128), I32),
-            DMA((3,)),
-        ],
-        compiler_params=pltpu.CompilerParams(vmem_limit_bytes=40 << 20),
-        name="owner",
-    )(qall, mall, pool)
-
+    po, ps = owner_call(nz, qall, mall, pool)
     return pl.pallas_call(
         functools.partial(return_kernel, nz, ntp),
         out_shape=(
@@ -435,7 +482,7 @@
         ]
         + [DMA((PLANE - 1,))] * 4 + [DMA((nz - 1,))] * 4 + [DMA((ntp - 1,))] * 2 + [DMA((1,))],
         compiler_params=pltpu.CompilerParams(
-            collective_id=1, has_side_effects=True, vmem_limit_bytes=24 << 20
+            collective_id=1, has_side_effects=True, vmem_limit_bytes=12 << 20
         ),
         name="give_back",
     )(po, ps, queries, fresh_key_value, o_weight, resid_in, norm_gain.reshape(1, width))

time: 117 us -> 88.3 us (0.75)
  Pallas kernels: 111 us -> 81.7 us
    pallas_call x1, Pallas kernels: 45.7 us -> 18.8 us  [owner_call(): pl.pallas_call(functools.partial(owner_kernel, nz, pool.shape[0]), out_sh...]
    pallas_call x1, Pallas kernels: 32.1 us -> 30.8 us  [body(): pl.pallas_call(functools.partial(return_kernel, nz, ntp), out_shape=(jax....]
    pallas_call x1, Pallas kernels: 33.3 us -> 32.1 us  [body(): pl.pallas_call(functools.partial(dispatch_kernel, nz), out_shape=(jax.Sha...]
    unnamed x18 -> x22, local copies, waits for them, and re-layouts: 4.62 us -> 5.66 us
where the time goes in v2:
time: 88.3 us; the launch traced here: 88.1 us
  Pallas kernels  81.7 us (93%)
  local copies, waits for them, and re-layouts  5.67 us (6%)
    pallas_call x1, Pallas kernels, body(): pl.pallas_call(functools.partial(dispatch_kernel, nz), out_shape=(jax.Sha...  32.1 us
    pallas_call x1, Pallas kernels, body(): pl.pallas_call(functools.partial(return_kernel, nz, ntp), out_shape=(jax....  30.8 us
    pallas_call x1, Pallas kernels, owner_call(): pl.pallas_call(functools.partial(owner_kernel, nz, pool.shape[0]), out_sh...  18.8 us
    unnamed x22, local copies, waits for them, and re-layouts  5.66 us

profile of v2, /device:TPU:1, one launch (start us, length us, event | category | flops | bytes accessed | tf_op | source)
XLA Modules:
  0.0 88.1 jit_solution(5864677777165519199)
XLA Ops:
  0.6 0.0 copy-start
  0.6 0.0 copy-start.3
  0.7 0.8 copy-done.3
  1.5 0.0 copy-start.5
  1.5 0.7 copy-done.5
  2.2 0.0 copy-start.6
  2.2 0.7 copy-done.6
  2.8 0.0 copy-start.8
  2.8 0.7 copy-done.8
  3.5 32.1 %dispatch.1 = (bf16[8,16,16,128]{3,2,1,0:T(8,128)(2,1)S(1)}, bf16[8,16,128]{2,1,0:T(8,128)(2,1)S(1)}) custom-call(bf16[4,512]{1,0:T(4,128)(2,1)S(1)} %copy-done.3, s32[4,128]{1,0:T(4,128)S(1)} %bitcast.2, s32[4,128]{1,0:T(4,128)S(1)} %bitcast.3, s32[4]{0:T(128)S(1)} %copy-done.8), custom_call_target="tpu_custom_call" | custom-call | tf_op jit(solution)/shard_map/dispatch/pallas_call | solution.py:449
  35.6 0.0 copy-start.1
  35.6 1.6 %copy-done.1 = bf16[64,128,128]{2,1,0:T(8,128)(2,1)S(1)} copy-done((bf16[64,128,128]{2,1,0:T(8,128)(2,1)S(1)}, bf16[64,128,128]{2,1,0:T(8,128)(2,1)}, u32[]{:S(2)}) %copy-start.1) | copy-done | bytes 2097176
  37.2 0.0 copy-start.9
  37.2 0.0 copy-start.2
  37.2 0.0 copy-start.4
  37.2 0.0 copy-start.7
  37.2 18.8 %owner.1 = (bf16[8,16,16,128]{3,2,1,0:T(8,128)(2,1)S(1)}, f32[8,8,128]{2,1,0:T(8,128)S(1)}) custom-call(bf16[8,16,16,128]{3,2,1,0:T(8,128)(2,1)S(1)} %get-tuple-element.6.qall_ref, bf16[8,16,128]{2,1,0:T(8,128)(2,1)S(1)} %get-tuple-element.7.mall_ref, bf16[64,128,128]{2,1,0:T(8,128)(2,1)S(1)} %copy-done.1), custom_call_target="tpu_custom_call" | custom-call | tf_op jit(solution)/shard_map/owner/pallas_call | solution.py:425
  56.0 0.0 copy-done.9
  56.0 0.0 copy-done
  56.1 0.0 copy-done.2
  56.1 0.0 copy-done.4
  56.1 0.0 copy-done.7
  56.1 30.8 %give_back.1 = (bf16[4,2048]{1,0:T(4,128)(2,1)S(1)}, bf16[4,2048]{1,0:T(4,128)(2,1)S(1)}) custom-call(bf16[8,16,16,128]{3,2,1,0:T(8,128)(2,1)S(1)} %get-tuple-element.8.po_ref, f32[8,8,128]{2,1,0:T(8,128)S(1)} %get-tuple-element.9.ps_ref, bf16[4,512]{1,0:T(4,128)(2,1)S(1)} %copy-done.4, bf16[4,128]{1,0:T(4,128)(2,1)S(1)} %copy-done.7, ...), custom_call_target="tpu_custom_call" | custom-call | tf_op jit(solution)/shard_map/give_back/pallas_call | solution.py:469
  86.9 0.6 copy.13
  87.5 0.6 copy.14
  (1 shorter events, 0.0 us)
Async XLA Ops:
  0.6 55.4 %copy-start = (bf16[512,2048]{1,0:T(8,128)(2,1)S(1)}, bf16[512,2048]{1,0:T(8,128)(2,1)}, u32[]{:S(2)}) copy-start(bf16[512,2048]{1,0:T(8,128)(2,1)} %w_hbm.1) | copy-start | bytes 6291460
  0.6 0.8 copy-start.3
  1.5 0.7 copy-start.5
  2.2 0.7 copy-start.6
  2.8 0.7 copy-start.8
  35.6 1.6 %copy-start.1 = (bf16[64,128,128]{2,1,0:T(8,128)(2,1)S(1)}, bf16[64,128,128]{2,1,0:T(8,128)(2,1)}, u32[]{:S(2)}) copy-start(bf16[64,128,128]{2,1,0:T(8,128)(2,1)} %pool.1) | copy-start | bytes 6291460
  37.2 18.9 %copy-start.9 = (bf16[2048]{0:T(1024)(128)(2,1)S(1)}, bf16[2048]{0:T(1024)(128)(2,1)}, u32[]{:S(2)}) copy-start(bf16[2048]{0:T(1024)(128)(2,1)} %param.17) | copy-start | bytes 12292
  37.2 18.9 %copy-start.2 = (bf16[4,2048]{1,0:T(4,128)(2,1)S(1)}, bf16[4,2048]{1,0:T(4,128)(2,1)}, u32[]{:S(2)}) copy-start(bf16[4,2048]{1,0:T(4,128)(2,1)} %resid_ref.1) | copy-start | bytes 49156
  37.2 18.9 %copy-start.4 = (bf16[4,512]{1,0:T(4,128)(2,1)S(1)}, bf16[4,512]{1,0:T(4,128)(2,1)}, u32[]{:S(2)}) copy-start(bf16[4,512]{1,0:T(4,128)(2,1)} %q_ref.3) | copy-start | bytes 12292
  37.2 18.9 %copy-start.7 = (bf16[4,128]{1,0:T(4,128)(2,1)S(1)}, bf16[4,128]{1,0:T(4,128)(2,1)}, u32[]{:S(2)}) copy-start(bf16[4,128]{1,0:T(4,128)(2,1)} %fresh_ref.1) | copy-start | bytes 3076

commit v3 on v2

--- a/solution.py
+++ b/solution.py
@@ -39,80 +39,25 @@
     )
 
 
-def dispatch_kernel(
-    nz, q_ref, owner_ref, page_ref, len_ref, qall_ref, mall_ref,
-    zq, zsend, zm, ysend, qs_z, qr_z, ms_z, mr_z, qs_y, qr_y, ms_y, mr_y,
-):
-    me = lax.axis_index("req")
-    z, yc = me // PLANE, me % PLANE
-    zpeers = [(z + k) % nz for k in range(1, nz)]
-    ypeers = [(yc + k) % PLANE for k in range(1, PLANE)]
-    barrier = pltpu.get_barrier_semaphore()
-    for p in zpeers:
-        pl.semaphore_signal(barrier, inc=1, device_id={"req": p * PLANE + yc}, device_id_type=MESH)
-    for p in ypeers:
-        pl.semaphore_signal(barrier, inc=1, device_id={"req": z * PLANE + p}, device_id_type=MESH)
-
-    zq[z] = head_pair_rows(q_ref[...].astype(F32)).astype(BF16)
-    rows, lanes = iota((128, 128), 0), iota((128, 128), 1)
-    tri = jnp.where(rows <= lanes, 1.0, 0.0).astype(BF16)
-    ones = jnp.ones((128, 128), BF16)
-    base = jnp.zeros((128, 128), F32)
-    table = jnp.zeros((128, 128), F32)
-    for s in range(SLOTS):
-        live = jnp.clip(len_ref[s] - iota((1, 128), 1) * 128, 0, 128)
-        hit = jnp.logical_and(rows == owner_ref[s : s + 1, :], live > 0)
-        hot = jnp.where(hit, 1.0, 0.0).astype(BF16)
-        rank = jnp.sum(jnp.where(hit, base + dot_nn(hot, tri) - 1.0, 0.0), axis=0, keepdims=True)
-        base = base + dot_nn(hot, ones)
-        kind = rows // CAP
-        val = jnp.where(
-            kind == 0, page_ref[s : s + 1, :].astype(F32),
-            jnp.where(kind == 1, live.astype(F32), jnp.where(kind == 2, float(s), 0.0)),
-        )
-        place = jnp.where((rows % CAP).astype(F32) == rank, val, 0.0).astype(BF16)
-        table = table + dot_nt(hot, place)
-    zsend[...] = table.reshape(nz, PLANE, 128).astype(BF16)
-    zm[z] = zsend[z]
-
-    pl.semaphore_wait(barrier, nz - 1 + PLANE - 1)
-    copies = []
-    for i, p in enumerate(zpeers):
-        to = {"req": p * PLANE + yc}
-        copies.append(remote(zq.at[z], zq.at[z], qs_z.at[i], qr_z.at[i], to))
-        copies.append(remote(zsend.at[p], zm.at[z], ms_z.at[i], mr_z.at[i], to))
+def start_all(copies):
     for c in copies:
         c.start()
+
+
+def wait_all(copies):
     for c in copies:
         c.wait()
-    got = zm[...].astype(F32)
-    for d in range(PLANE):
-        ysend[d] = jnp.concatenate([got[i, d : d + 1, :] for i in range(nz)], axis=0).astype(BF16)
-    qall_ref[yc] = zq[...]
-    mall_ref[yc] = ysend[yc]
-    copies = []
-    for i, p in enumerate(ypeers):
-        to = {"req": z * PLANE + p}
-        copies.append(remote(zq, qall_ref.at[yc], qs_y.at[i], qr_y.at[i], to))
-        copies.append(remote(ysend.at[p], mall_ref.at[yc], ms_y.at[i], mr_y.at[i], to))
-    for c in copies:
-        c.start()
-    for c in copies:
-        c.wait()
-
-
-def owner_kernel(
-    nz, npages, qall_ref, mall_ref, pool, po_ref, ps_ref,
-    qx, o_s, ml_s, wn_s, sg_s, s0, s1, p0, p1, lst_v, lst, sems,
-):
-    nsrc = nz * PLANE
-    row8, lane8 = iota((8, 128), 0), iota((8, 128), 1)
-    low, left = row8 < 4, lane8 < 64
-    meta_b = mall_ref[...].reshape(nsrc, 128)
+
+
+def far_first(n):
+    return sorted(range(1, n), key=lambda k: -min(k, n - k))
+
+
+def sort_items(nsrc, npages, meta_b, lists_ref, items_ref, slots_ref):
     meta = meta_b.astype(F32).T
     page, live, slot = meta[0:8], meta[8:16], meta[16:24]
-    valid = live > 0.0
-
+    items_ref[0:8] = live
+    items_ref[8:16] = slot
     prow = iota((npages, 128), 0).astype(F32)
     eqs = [
         jnp.where(jnp.logical_and(prow == page[r : r + 1], live[r : r + 1] > 0.0), 1.0, 0.0) for r in range(CAP)
@@ -143,14 +88,113 @@
         col = jnp.where(crow == chunk, 1.0, 0.0)
         lists = lists + dot_nt(jnp.concatenate(pick, axis=0).astype(BF16), col.astype(BF16))
     srcs, nth = lists[0:CHUNK], lists[CHUNK : 2 * CHUNK]
-    lst_v[0:16] = (srcs * SLOTS + lists[3 * CHUNK : 4 * CHUNK]).astype(I32)
-    lst_v[16:32] = jnp.where(nth > 0.0, srcs * CAP + nth - 1.0, float(nsrc * CAP)).astype(I32)
-    lst_v[32:48] = lists[2 * CHUNK : 3 * CHUNK].astype(I32)
-    lst_v[48:56] = jnp.concatenate(
+    lists_ref[0:16] = (srcs * SLOTS + lists[3 * CHUNK : 4 * CHUNK]).astype(I32)
+    lists_ref[16:32] = jnp.where(nth > 0.0, srcs * CAP + nth - 1.0, float(nsrc * CAP)).astype(I32)
+    lists_ref[32:48] = lists[2 * CHUNK : 3 * CHUNK].astype(I32)
+    lists_ref[48:56] = jnp.concatenate(
         [lists[4 * CHUNK : 4 * CHUNK + 1], total, jnp.zeros((6, 128), F32)], axis=0
     ).astype(I32)
-    lst_copy = pltpu.make_async_copy(lst_v, lst, sems.at[0])
+    spread = jnp.where(iota((128, 128), 0) == 2 * CAP + iota((128, 128), 1) // 8 % CAP, 1.0, 0.0).astype(BF16)
+    slots_ref[...] = dot_nn(meta_b, spread)
+
+
+def dispatch_kernel(
+    nz, npages, q_hbm, owner_hbm, page_hbm, len_hbm, qall_ref, lists_ref, items_ref, slots_ref,
+    q_v, owner_v, page_v, len_s, zq, zsend, zm, ysend, mall,
+    in_sem, qs_z, qr_z, ms_z, mr_z, qs_y, qr_y, qs_c, qr_c, ms_y, mr_y,
+):
+    me = lax.axis_index("req")
+    z, yc = me // PLANE, me % PLANE
+    y, core = yc // 2, yc % 2
+    sib = yc + 1 - 2 * core
+    zpeers = [(z + k) % nz for k in far_first(nz)]
+    plane = [(yc + k) % PLANE for k in range(1, PLANE)]
+    ypeers = [(y + k) % 4 for k in (2, 1, 3)]
+    barrier = pltpu.get_barrier_semaphore()
+    for p in zpeers:
+        pl.semaphore_signal(barrier, inc=1, device_id={"req": p * PLANE + yc}, device_id_type=MESH)
+    for p in plane:
+        pl.semaphore_signal(barrier, inc=1, device_id={"req": z * PLANE + p}, device_id_type=MESH)
+    ins = [
+        pltpu.make_async_copy(h, v, in_sem.at[i])
+        for i, (h, v) in enumerate([(q_hbm, q_v), (owner_hbm, owner_v), (page_hbm, page_v), (len_hbm, len_s)])
+    ]
+    start_all(ins)
+    ins[0].wait()
+    zq[z] = head_pair_rows(q_v[...].astype(F32)).astype(BF16)
+    pl.semaphore_wait(barrier, nz - 1 + PLANE - 1)
+    q_z = [
+        remote(zq.at[z], zq.at[z], qs_z.at[i], qr_z.at[i], {"req": p * PLANE + yc}) for i, p in enumerate(zpeers)
+    ]
+    start_all(q_z)
+
+    wait_all(ins[1:])
+    rows, lanes = iota((128, 128), 0), iota((128, 128), 1)
+    tri = jnp.where(rows <= lanes, 1.0, 0.0).astype(BF16)
+    ones = jnp.ones((128, 128), BF16)
+    base = jnp.zeros((128, 128), F32)
+    table = jnp.zeros((128, 128), F32)
+    for s in range(SLOTS):
+        live = jnp.clip(len_s[s] - iota((1, 128), 1) * 128, 0, 128)
+        hit = jnp.logical_and(rows == owner_v[s : s + 1, :], live > 0)
+        hot = jnp.where(hit, 1.0, 0.0).astype(BF16)
+        rank = jnp.sum(jnp.where(hit, base + dot_nn(hot, tri) - 1.0, 0.0), axis=0, keepdims=True)
+        base = base + dot_nn(hot, ones)
+        kind = rows // CAP
+        val = jnp.where(
+            kind == 0, page_v[s : s + 1, :].astype(F32),
+            jnp.where(kind == 1, live.astype(F32), jnp.where(kind == 2, float(s), 0.0)),
+        )
+        place = jnp.where((rows % CAP).astype(F32) == rank, val, 0.0).astype(BF16)
+        table = table + dot_nt(hot, place)
+    zsend[...] = table.reshape(nz, PLANE, 128).astype(BF16)
+    zm[z] = zsend[z]
+    m_z = [
+        remote(zsend.at[p], zm.at[z], ms_z.at[i], mr_z.at[i], {"req": p * PLANE + yc}) for i, p in enumerate(zpeers)
+    ]
+    start_all(m_z)
+
+    wait_all(q_z)
+    q_y = [
+        remote(zq, qall_ref.at[yc], qs_y.at[i], qr_y.at[i], {"req": z * PLANE + 2 * p + core})
+        for i, p in enumerate(ypeers)
+    ]
+    q_c = [remote(zq, qall_ref.at[yc], qs_c.at[3], qr_c.at[3], {"req": z * PLANE + sib})]
+    start_all(q_y + q_c)
+    qall_ref[yc] = zq[...]
+
+    wait_all(m_z)
+    got = zm[...].astype(F32)
+    for d in range(PLANE):
+        ysend[d] = jnp.concatenate([got[i, d : d + 1, :] for i in range(nz)], axis=0).astype(BF16)
+    mall[yc] = ysend[yc]
+    m_y = [
+        remote(ysend.at[p], mall.at[yc], ms_y.at[i], mr_y.at[i], {"req": z * PLANE + p}) for i, p in enumerate(plane)
+    ]
+    start_all(m_y)
+    wait_all(m_y)
+    sort_items(nz * PLANE, npages, mall[...].reshape(nz * PLANE, 128), lists_ref, items_ref, slots_ref)
+    for i, p in enumerate((2, 3, 1)):
+        q_y[i].wait()
+        slot = (y + p) % 4 * 2 + core
+        c = remote(qall_ref.at[slot], qall_ref.at[slot], qs_c.at[i], qr_c.at[i], {"req": z * PLANE + sib})
+        c.start()
+        q_c.append(c)
+    wait_all(q_c)
+
+
+def owner_kernel(
+    nz, qall_ref, lists_ref, items_ref, sg_s, pool_hbm, po_ref, ps_ref,
+    pool, qx, o_s, ml_s, wn_s, s0, s1, p0, p1, lst, sems,
+):
+    nsrc = nz * PLANE
+    lst_copy = pltpu.make_async_copy(lists_ref, lst, sems.at[0])
     lst_copy.start()
+    pool_copy = pltpu.make_async_copy(pool_hbm, pool, sems.at[1])
+    pool_copy.start()
+    row8, lane8 = iota((8, 128), 0), iota((8, 128), 1)
+    low, left = row8 < 4, lane8 < 64
+    live, slot = items_ref[0:8], items_ref[8:16]
 
     keep = jnp.where(left, 0.125, 0.0)
     group = 8
@@ -166,9 +210,8 @@
                 qx[i * SLOTS + 2 * t] = jnp.where(low, v, pltpu.roll(vs, 64, 1)) * keep
                 qx[i * SLOTS + 2 * t + 1] = jnp.where(low, vs, pltpu.roll(v, 64, 1)) * keep
 
-    spread = jnp.where(iota((128, 128), 0) == 2 * CAP + iota((128, 128), 1) // 8 % CAP, 1.0, 0.0).astype(BF16)
-    sg_s[...] = dot_nn(meta_b, spread)
     lst_copy.wait()
+    pool_copy.wait()
 
     def scores_of(c, out):
         c = jnp.clip(c, 0, 127)
@@ -278,39 +321,58 @@
                 po_ref[d, 2 * j + a] = jnp.where(left16, pltpu.roll(even, 64, 1), odd).astype(BF16)
 
 
+def spread_weights(x, nz):
+    low = iota((8, 128), 0) < 4
+    xs = pltpu.roll(x, 4, 0)
+    yl = jnp.where(low, x, pltpu.roll(xs, 128 - nz, 1))
+    yr = jnp.where(low, xs, pltpu.roll(x, 128 - nz, 1))
+    return yl, yr
+
+
 def return_kernel(
-    nz, ntp, po_ref, ps_ref, q_ref, fresh_ref, w_hbm, resid_ref, gain_ref, res_out, norm_out,
-    ro, rs, wn, acc, o1, s1, ro2, rs2, wv, parts,
-    os_y, or_y, ss_y, sr_y, os_z, or_z, ss_z, sr_z, ts, tr, wsem,
+    nz, ntp, po_ref, ps_ref, q_hbm, fresh_hbm, w_hbm, resid_hbm, gain_hbm, res_out, norm_out,
+    q_ref, fresh_ref, wv, resid_ref, gain_ref, rc, rsc, ysnd, ystat, ry, rsy, o1, s1, ro2, rs2, parts,
+    in_sem, os_c, or_c, ss_c, sr_c, os_y, or_y, ss_y, sr_y, os_z, or_z, ss_z, sr_z, ts, tr,
 ):
     me, tp = lax.axis_index("req"), lax.axis_index("tp")
     z, yc = me // PLANE, me % PLANE
-    zpeers = [(z + k) % nz for k in range(1, nz)]
-    ypeers = [(yc + k) % PLANE for k in range(1, PLANE)]
+    y, core = yc // 2, yc % 2
+    sib = yc + 1 - 2 * core
+    zpeers = [(z + k) % nz for k in far_first(nz)]
+    yorder = [(y + k) % 4 for k in (2, 1, 3, 0)]
     tpeers = [(tp + k) % ntp for k in range(1, ntp)]
     barrier = pltpu.get_barrier_semaphore()
+    pl.semaphore_signal(barrier, inc=1, device_id={"req": z * PLANE + sib}, device_id_type=MESH)
+    for p in yorder[:3]:
+        pl.semaphore_signal(barrier, inc=1, device_id={"req": z * PLANE + 2 * p + core}, device_id_type=MESH)
     for p in zpeers:
         pl.semaphore_signal(barrier, inc=1, device_id={"req": p * PLANE + yc}, device_id_type=MESH)
-    for p in ypeers:
-        pl.semaphore_signal(barrier, inc=1, device_id={"req": z * PLANE + p}, device_id_type=MESH)
     for p in tpeers:
         pl.semaphore_signal(barrier, inc=1, device_id={"tp": p}, device_id_type=MESH)
-    w_copy = pltpu.make_async_copy(w_hbm, wv, wsem.at[0])
-    w_copy.start()
-    ro[yc] = po_ref[yc]
-    rs[yc] = ps_ref[yc]
-    pl.semaphore_wait(barrier, nz - 1 + PLANE - 1 + ntp - 1)
-
-    copies = []
-    for i, p in enumerate(ypeers):
-        to = {"req": z * PLANE + p}
-        copies.append(remote(po_ref.at[p], ro.at[yc], os_y.at[i], or_y.at[i], to))
-        copies.append(remote(ps_ref.at[p], rs.at[yc], ss_y.at[i], sr_y.at[i], to))
-    for c in copies:
-        c.start()
+    ins = [
+        pltpu.make_async_copy(h, v, in_sem.at[i])
+        for i, (h, v) in enumerate(
+            [(q_hbm, q_ref), (fresh_hbm, fresh_ref), (w_hbm, wv), (resid_hbm, resid_ref), (gain_hbm, gain_ref)]
+        )
+    ]
+    start_all(ins)
+    pl.semaphore_wait(barrier, nz - 1 + 4 + ntp - 1)
+
+    cores = []
+    for i, p in enumerate(yorder):
+        to = {"req": z * PLANE + sib}
+        theirs = 2 * p + 1 - core
+        cores.append(
+            [
+                remote(ps_ref.at[theirs], rsc.at[i], ss_c.at[i], sr_c.at[i], to),
+                remote(po_ref.at[theirs], rc.at[i], os_c.at[i], or_c.at[i], to),
+            ]
+        )
+        start_all(cores[-1])
 
     row8, lane8 = iota((8, 128), 0), iota((8, 128), 1)
     low, left = row8 < 4, lane8 < 64
+    wait_all(ins[:2])
     q16 = head_pair_rows(q_ref[...].astype(F32))
     fresh = fresh_ref[...].astype(F32)
     self_score, self_value = [], []
@@ -323,37 +385,54 @@
         self_score.append(jnp.where(left, ls, rsum) * 0.125)
         self_value.append(jnp.where(left, other, kv))
 
-    for c in copies:
-        c.wait()
-
-    stats = [rs[p] for p in range(PLANE)]
+    ys = []
+    for i, p in enumerate(yorder):
+        wait_all(cores[i])
+        ours = 2 * p + core
+        sa, sb = ps_ref[ours], rsc[i]
+        top = jnp.maximum(sa, sb)
+        ea, eb = jnp.exp(sa - top), jnp.exp(sb - top)
+        both = ea + eb
+        ystat[i] = top + jnp.log(both)
+        yl, yr = spread_weights(ea / both, nz)
+        for zi in range(nz):
+            halves = []
+            pa, pb = po_ref[ours, zi].astype(F32), rc[i, zi].astype(F32)
+            for t in range(2):
+                li = 2 * t * nz + zi
+                w = jnp.where(left, yl[:, li : li + 1], yr[:, li : li + 1])
+                b = pb[8 * t : 8 * t + 8]
+                halves.append(b + w * (pa[8 * t : 8 * t + 8] - b))
+            ysnd[i, zi] = jnp.concatenate(halves, axis=0).astype(BF16)
+        if i < 3:
+            to = {"req": z * PLANE + 2 * p + core}
+            ys.append(remote(ystat.at[i], rsy.at[i], ss_y.at[i], sr_y.at[i], to))
+            ys.append(remote(ysnd.at[i], ry.at[i], os_y.at[i], or_y.at[i], to))
+            start_all(ys[-2:])
+    wait_all(ys)
+
+    stats = [rsy[p] for p in range(3)] + [ystat[3]]
     top = stats[0]
-    for p in range(1, PLANE):
+    for p in range(1, 4):
         top = jnp.maximum(top, stats[p])
     ws = [jnp.exp(s - top) for s in stats]
     wsum = ws[0]
-    for p in range(1, PLANE):
+    for p in range(1, 4):
         wsum = wsum + ws[p]
-    for p in range(PLANE):
-        wn[p] = ws[p] / wsum
     lse = top + jnp.log(wsum)
-    acc[...] = jnp.zeros_like(acc)
-
-    def add_part(p, carry):
-        x = wn[p]
-        xs = pltpu.roll(x, 4, 0)
-        yl = jnp.where(low, x, pltpu.roll(xs, 128 - nz, 1))
-        yr = jnp.where(low, xs, pltpu.roll(x, 128 - nz, 1))
-        for zi in range(nz):
-            part = ro[p, zi].astype(F32)
-            for t in range(2):
-                li = 2 * t * nz + zi
+    sides = [spread_weights(w / wsum, nz) for w in ws]
+    for zi in range(nz):
+        pieces = [ry[p, zi].astype(F32) for p in range(3)] + [ysnd[3, zi].astype(F32)]
+        halves = []
+        for t in range(2):
+            li = 2 * t * nz + zi
+            total = jnp.zeros((8, 128), F32)
+            for p in range(4):
+                yl, yr = sides[p]
                 w = jnp.where(left, yl[:, li : li + 1], yr[:, li : li + 1])
-                acc[zi, 8 * t : 8 * t + 8] = acc[zi, 8 * t : 8 * t + 8] + w * part[8 * t : 8 * t + 8]
-        return carry
-
-    lax.fori_loop(0, PLANE, add_part, 0)
-    o1[...] = acc[...].astype(BF16)
+                total = total + w * pieces[p][8 * t : 8 * t + 8]
+            halves.append(total)
+        o1[zi] = jnp.concatenate(halves, axis=0).astype(BF16)
     by_slot = [pltpu.roll(lse, (128 - nz * s) % 128, 1) if s else lse for s in range(SLOTS)]
     rows = jnp.concatenate(by_slot + [jnp.zeros((96, 128), F32)], axis=0).T
     for zi in range(nz):
@@ -395,7 +474,7 @@
     wide = jnp.concatenate([jnp.where(r16 % 4 == h, att, 0.0) for h in range(4)], axis=1).astype(BF16)
     sel = jnp.where(iota((16, 16), 1) // 4 == iota((16, 16), 0), 1.0, 0.0).astype(BF16)
     lhs = dot_nn(sel, wide).astype(BF16)
-    w_copy.wait()
+    wait_all(ins[2:])
     parts[tp] = dot_nn(lhs, wv[...])[0:SLOTS]
     copies = []
     for i, p in enumerate(tpeers):
@@ -417,75 +496,95 @@
     return [pl.BlockSpec(memory_space=pltpu.VMEM)] * n
 
 
-ANY = pl.BlockSpec(memory_space=pl.ANY)
-
-
-def owner_call(nz, qall, mall, pool):
+def in_hbm(x):
+    return pltpu.with_memory_space_constraint(x, pltpu.HBM)
+
+
+def hbm(n):
+    return [pl.BlockSpec(memory_space=pltpu.HBM)] * n
+
+
+def owner_call(nz, qall, lists, items, slots, pool):
     nsrc = nz * PLANE
     return pl.pallas_call(
-        functools.partial(owner_kernel, nz, pool.shape[0]),
+        functools.partial(owner_kernel, nz),
         out_shape=(
             jax.ShapeDtypeStruct((PLANE, nz, 16, 128), BF16),
             jax.ShapeDtypeStruct((PLANE, 8, 128), F32),
         ),
-        in_specs=vmem(3),
+        in_specs=vmem(4) + hbm(1),
         out_specs=tuple(vmem(2)),
         scratch_shapes=[
+            VM(pool.shape, BF16),
             VM((nsrc * SLOTS, 8, 128), F32),
             VM((nsrc * CAP + 1, 8, 128), F32), VM((nsrc * CAP + 1, 8, 128), F32),
-            VM((CAP, 8, 128), F32), VM((nsrc, 128), F32),
+            VM((CAP, 8, 128), F32),
             VM((128, 128), F32), VM((128, 128), F32), VM((128, 128), BF16), VM((128, 128), BF16),
-            VM((56, 128), I32), pltpu.SMEM((56, 128), I32),
-            pltpu.SemaphoreType.DMA((1,)),
+            pltpu.SMEM((56, 128), I32),
+            pltpu.SemaphoreType.DMA((2,)),
         ],
-        compiler_params=pltpu.CompilerParams(vmem_limit_bytes=20 << 20),
+        compiler_params=pltpu.CompilerParams(vmem_limit_bytes=24 << 20),
         name="owner",
-    )(qall, mall, pool)
-
-
-def body(nz, ntp, queries, fresh_key_value, pool, block_owner, block_page, lengths, o_weight, resid_in, norm_gain):
-    width = o_weight.shape[1]
+    )(qall, lists, items, slots, in_hbm(pool))
+
+
+def dispatch_call(nz, npages, queries, block_owner, block_page, lengths):
     DMA = pltpu.SemaphoreType.DMA
-    qall, mall = pl.pallas_call(
-        functools.partial(dispatch_kernel, nz),
+    return pl.pallas_call(
+        functools.partial(dispatch_kernel, nz, npages),
         out_shape=(
             jax.ShapeDtypeStruct((PLANE, nz, 16, 128), BF16),
-            jax.ShapeDtypeStruct((PLANE, nz, 128), BF16),
+            jax.ShapeDtypeStruct((56, 128), I32),
+            jax.ShapeDtypeStruct((16, 128), F32),
+            jax.ShapeDtypeStruct((nz * PLANE, 128), F32),
         ),
-        in_specs=vmem(3) + [pl.BlockSpec(memory_space=pltpu.SMEM)],
-        out_specs=tuple(vmem(2)),
+        in_specs=hbm(4),
+        out_specs=tuple(vmem(4)),
         scratch_shapes=[
+            VM(queries.shape, BF16), VM((SLOTS, 128), I32), VM((SLOTS, 128), I32), pltpu.SMEM((SLOTS,), I32),
             VM((nz, 16, 128), BF16), VM((nz, PLANE, 128), BF16), VM((nz, PLANE, 128), BF16),
-            VM((PLANE, nz, 128), BF16),
+            VM((PLANE, nz, 128), BF16), VM((PLANE, nz, 128), BF16),
         ]
-        + [DMA((nz - 1,))] * 4 + [DMA((PLANE - 1,))] * 4,
+        + [DMA((4,))] + [DMA((nz - 1,))] * 4 + [DMA((3,))] * 2 + [DMA((4,))] * 2 + [DMA((PLANE - 1,))] * 2,
         compiler_params=pltpu.CompilerParams(
             collective_id=0, has_side_effects=True, vmem_limit_bytes=6 << 20
         ),
         name="dispatch",
-    )(queries, block_owner.reshape(SLOTS, 128), block_page.reshape(SLOTS, 128), lengths)
-
-    po, ps = owner_call(nz, qall, mall, pool)
+    )(*map(in_hbm, (queries, block_owner.reshape(SLOTS, 128), block_page.reshape(SLOTS, 128), lengths)))
+
+
+def return_call(nz, ntp, po, ps, queries, fresh_key_value, o_weight, resid_in, norm_gain):
+    width = o_weight.shape[1]
+    DMA = pltpu.SemaphoreType.DMA
+    block = (nz, 16, 128)
     return pl.pallas_call(
         functools.partial(return_kernel, nz, ntp),
         out_shape=(
             jax.ShapeDtypeStruct((SLOTS, width), BF16),
             jax.ShapeDtypeStruct((SLOTS, width), BF16),
         ),
-        in_specs=vmem(4) + [ANY] + vmem(2),
+        in_specs=vmem(2) + hbm(5),
         out_specs=tuple(vmem(2)),
         scratch_shapes=[
-            VM((PLANE, nz, 16, 128), BF16), VM((PLANE, 8, 128), F32), VM((PLANE, 8, 128), F32),
-            VM((nz, 16, 128), F32), VM((nz, 16, 128), BF16), VM((nz, 1, 128), F32),
-            VM((nz, 16, 128), BF16), VM((nz, 1, 128), F32), VM(o_weight.shape, BF16),
+            VM(queries.shape, BF16), VM(fresh_key_value.shape, BF16), VM(o_weight.shape, BF16),
+            VM(resid_in.shape, BF16), VM((1, width), BF16),
+            VM((4,) + block, BF16), VM((4, 8, 128), F32), VM((4,) + block, BF16), VM((4, 8, 128), F32),
+            VM((3,) + block, BF16), VM((3, 8, 128), F32),
+            VM(block, BF16), VM((nz, 1, 128), F32), VM(block, BF16), VM((nz, 1, 128), F32),
             VM((ntp, SLOTS, width), F32),
         ]
-        + [DMA((PLANE - 1,))] * 4 + [DMA((nz - 1,))] * 4 + [DMA((ntp - 1,))] * 2 + [DMA((1,))],
+        + [DMA((5,))] + [DMA((4,))] * 4 + [DMA((3,))] * 4 + [DMA((nz - 1,))] * 4 + [DMA((ntp - 1,))] * 2,
         compiler_params=pltpu.CompilerParams(
             collective_id=1, has_side_effects=True, vmem_limit_bytes=12 << 20
         ),
         name="give_back",
-    )(po, ps, queries, fresh_key_value, o_weight, resid_in, norm_gain.reshape(1, width))
+    )(po, ps, *map(in_hbm, (queries, fresh_key_value, o_weight, resid_in, norm_gain.reshape(1, width))))
+
+
+def body(nz, ntp, queries, fresh_key_value, pool, block_owner, block_page, lengths, o_weight, resid_in, norm_gain):
+    qall, lists, items, slots = dispatch_call(nz, pool.shape[0], queries, block_owner, block_page, lengths)
+    po, ps = owner_call(nz, qall, lists, items, slots, pool)
+    return return_call(nz, ntp, po, ps, queries, fresh_key_value, o_weight, resid_in, norm_gain)
 
 
 def solution(mesh):

time: 88.3 us -> 78.6 us (0.89)
  Pallas kernels: 81.7 us -> 75 us
  local copies, waits for them, and re-layouts: 5.67 us -> 1.82 us
    pallas_call x3, Pallas kernels: 81.7 us -> 75 us  [the longest x1 31.9 us: dispatch_call(): pl.pallas_call(functools.partial(dispatch_kernel, nz, npages), out_shape=...]
    unnamed x22 -> x4, local copies, waits for them, and re-layouts: 5.66 us -> 1.22 us
where the time goes in v3:
time: 78.6 us; the launch traced here: 77.5 us
  Pallas kernels  75 us (95%)
  local copies, waits for them, and re-layouts  1.82 us (2%)
    pallas_call x1, Pallas kernels, dispatch_call(): pl.pallas_call(functools.partial(dispatch_kernel, nz, npages), out_shape=...  31.9 us
    pallas_call x1, Pallas kernels, return_call(): pl.pallas_call(functools.partial(return_kernel, nz, ntp), out_shape=(jax....  25.5 us
    pallas_call x1, Pallas kernels, owner_call(): pl.pallas_call(functools.partial(owner_kernel, nz), out_shape=(jax.ShapeD...  17.7 us

profile of v3, /device:TPU:1, one launch (start us, length us, event | category | flops | bytes accessed | tf_op | source)
XLA Modules:
  0.0 77.5 jit_solution(2942718647119237733)
XLA Ops:
  0.6 0.0 copy-start
  0.6 31.9 %dispatch.1 = (bf16[8,16,16,128]{3,2,1,0:T(8,128)(2,1)S(1)}, s32[56,128]{1,0:T(8,128)S(1)}, f32[16,128]{1,0:T(8,128)S(1)}, f32[128,128]{1,0:T(8,128)S(1)}) custom-call(bf16[4,512]{1,0:T(4,128)(2,1)} %q_hbm.3, s32[4,128]{1,0:T(4,128)} %bitcast.2, s32[4,128]{1,0:T(4,128)} %bitcast.3, s32[4]{0:T(128)} %len_hbm.1), custom_call_target="tpu_custom_call" | custom-call | tf_op jit(solution)/shard_map/dispatch/pallas_call | solution.py:533
  32.5 17.7 %owner.1 = (bf16[8,16,16,128]{3,2,1,0:T(8,128)(2,1)S(1)}, f32[8,8,128]{2,1,0:T(8,128)S(1)}) custom-call(bf16[8,16,16,128]{3,2,1,0:T(8,128)(2,1)S(1)} %get-tuple-element.8.qall_ref, s32[56,128]{1,0:T(8,128)S(1)} %get-tuple-element.9.lists_ref, f32[16,128]{1,0:T(8,128)S(1)} %get-tuple-element.10.items_ref, f32[128,128]{1,0:T(8,128)S(1)} %get-tuple-element.11.sg_s, ...), custom_call_target="tpu_custom_call" | custom-call | tf_op jit(solution)/shard_map/owner/pallas_call | solution.py:509
  50.2 0.0 copy-done
  50.2 0.6 reshape.15.gain_hbm
  50.8 25.5 %give_back.1 = (bf16[4,2048]{1,0:T(4,128)(2,1)S(1)}, bf16[4,2048]{1,0:T(4,128)(2,1)S(1)}) custom-call(bf16[8,16,16,128]{3,2,1,0:T(8,128)(2,1)S(1)} %get-tuple-element.12.po_ref, f32[8,8,128]{2,1,0:T(8,128)S(1)} %get-tuple-element.13.ps_ref, bf16[4,512]{1,0:T(4,128)(2,1)} %q_hbm.3, bf16[4,128]{1,0:T(4,128)(2,1)} %fresh_hbm.1, bf16[512,2048]{1,0:T(8,128)(2,1)} %w_hbm.1, ...), custom_call_target="tpu_custom_call" | custom-call | tf_op jit(solution)/shard_map/give_back/pallas_call | solution.py:560
  76.3 0.6 copy.13
  76.9 0.6 copy.14
Async XLA Ops:
  0.6 49.6 %copy-start = (bf16[2048]{0:T(1024)(128)(2,1)S(1)}, bf16[2048]{0:T(1024)(128)(2,1)}, u32[]{:S(2)}) copy-start(bf16[2048]{0:T(1024)(128)(2,1)} %param.17) | copy-start | bytes 12292

commit v4 on v3

--- a/solution.py
+++ b/solution.py
@@ -12,6 +12,8 @@
 NEG = -1e30
 CAP = 8
 CHUNK = 16
+UNROLL = 4
+COLUMNS = 128
 SLOTS = 4
 PLANE = 8
 VM = pltpu.VMEM
@@ -76,9 +78,9 @@
     total = (first + chunks)[npages - 1 : npages]
 
     krow = iota((CHUNK, 128), 0).astype(F32)
-    crow = iota((128, 128), 0).astype(F32)
+    crow = iota((COLUMNS, 128), 0).astype(F32)
     src = iota((1, 128), 1).astype(F32)
-    lists = jnp.zeros((5 * CHUNK, 128), F32)
+    lists = jnp.zeros((5 * CHUNK, COLUMNS), F32)
     for r in range(CAP):
         row = slice(r, r + 1)
         pos = jnp.sum(eqs[r] * (first * CHUNK + ranks[r] - 1.0), axis=0, keepdims=True)
@@ -88,11 +90,11 @@
         col = jnp.where(crow == chunk, 1.0, 0.0)
         lists = lists + dot_nt(jnp.concatenate(pick, axis=0).astype(BF16), col.astype(BF16))
     srcs, nth = lists[0:CHUNK], lists[CHUNK : 2 * CHUNK]
-    lists_ref[0:16] = (srcs * SLOTS + lists[3 * CHUNK : 4 * CHUNK]).astype(I32)
-    lists_ref[16:32] = jnp.where(nth > 0.0, srcs * CAP + nth - 1.0, float(nsrc * CAP)).astype(I32)
-    lists_ref[32:48] = lists[2 * CHUNK : 3 * CHUNK].astype(I32)
-    lists_ref[48:56] = jnp.concatenate(
-        [lists[4 * CHUNK : 4 * CHUNK + 1], total, jnp.zeros((6, 128), F32)], axis=0
+    lists_ref[0:CHUNK] = (srcs * SLOTS + lists[3 * CHUNK : 4 * CHUNK]).astype(I32)
+    lists_ref[CHUNK : 2 * CHUNK] = jnp.where(nth > 0.0, srcs * CAP + nth - 1.0, float(nsrc * CAP)).astype(I32)
+    lists_ref[2 * CHUNK : 3 * CHUNK] = lists[2 * CHUNK : 3 * CHUNK].astype(I32)
+    lists_ref[3 * CHUNK : 3 * CHUNK + 8] = jnp.concatenate(
+        [lists[4 * CHUNK : 4 * CHUNK + 1], jnp.tile(total, (1, COLUMNS // 128)), jnp.zeros((6, COLUMNS), F32)], axis=0
     ).astype(I32)
     spread = jnp.where(iota((128, 128), 0) == 2 * CAP + iota((128, 128), 1) // 8 % CAP, 1.0, 0.0).astype(BF16)
     slots_ref[...] = dot_nn(meta_b, spread)
@@ -185,7 +187,7 @@
 
 def owner_kernel(
     nz, qall_ref, lists_ref, items_ref, sg_s, pool_hbm, po_ref, ps_ref,
-    pool, qx, o_s, ml_s, wn_s, s0, s1, p0, p1, lst, sems,
+    pool, qx, o_s, ml_s, wn_s, s0, p0, lst, sems,
 ):
     nsrc = nz * PLANE
     lst_copy = pltpu.make_async_copy(lists_ref, lst, sems.at[0])
@@ -204,6 +206,8 @@
         for u in range(group):
             i = g * group + u
             q = qall_ref[i // nz, i % nz].astype(F32)
+            for r in range(CAP):
+                o_s[i * CAP + r] = jnp.zeros((8, 128), F32)
             for t in range(2):
                 v = q[8 * t : 8 * t + 8]
                 vs = pltpu.roll(v, 4, 0)
@@ -214,38 +218,38 @@
     pool_copy.wait()
 
     def scores_of(c, out):
-        c = jnp.clip(c, 0, 127)
+        c = jnp.clip(c, 0, COLUMNS - 1)
         q = jnp.concatenate([qx[lst[k, c]] for k in range(CHUNK)], axis=0).astype(BF16)
-        out[...] = dot_nt(q, pool[lst[48, c]])
+        out[...] = dot_nt(q, pool[lst[3 * CHUNK, c]])
 
     def probs_of(c, scores, out):
-        c = jnp.clip(c, 0, 127)
+        c = jnp.clip(c, 0, COLUMNS - 1)
         pair = []
         for k in range(CHUNK):
-            sc = jnp.where(lane8 < lst[32 + k, c], scores[8 * k : 8 * k + 8], NEG)
+            sc = jnp.where(lane8 < lst[2 * CHUNK + k, c], scores[8 * k : 8 * k + 8], NEG)
             top = jnp.max(sc, axis=1, keepdims=True)
             pr = jnp.exp(sc - top)
-            ml_s[lst[16 + k, c]] = jnp.where(left, top, jnp.sum(pr, axis=1, keepdims=True))
+            ml_s[lst[CHUNK + k, c]] = jnp.where(left, top, jnp.sum(pr, axis=1, keepdims=True))
             pair.append(pr)
             if k % 2:
                 out[8 * k - 8 : 8 * k + 8] = jnp.concatenate(pair, axis=0).astype(BF16)
                 pair = []
 
     def values_of(c, probs):
-        c = jnp.clip(c, 0, 127)
-        out = dot_nn(probs[...], pool[lst[48, c]])
+        c = jnp.clip(c, 0, COLUMNS - 1)
+        out = dot_nn(probs[...], pool[lst[3 * CHUNK, c]])
         for k in range(CHUNK):
-            o_s[lst[16 + k, c]] = out[8 * k : 8 * k + 8]
-
-    @pl.loop(0, (lst[49, 0] + 3) // 2)
+            o_s[lst[CHUNK + k, c]] = out[8 * k : 8 * k + 8]
+
+    @pl.loop(0, (lst[3 * CHUNK + 1, 0] + UNROLL - 1) // UNROLL + 2)
     def _(step):
-        c = 2 * step
-        scores_of(c, s0)
-        probs_of(c - 1, s1, p1)
-        values_of(c - 2, p0)
-        scores_of(c + 1, s1)
-        probs_of(c, s0, p0)
-        values_of(c - 1, p1)
+        c = step * UNROLL
+        for u in range(UNROLL):
+            values_of(c - 2 * UNROLL + u, p0.at[u])
+        for u in range(UNROLL):
+            probs_of(c - UNROLL + u, s0.at[u], p0.at[u])
+        for u in range(UNROLL):
+            scores_of(c + u, s0.at[u])
 
     halves = []
     for h in range(2):
@@ -284,11 +288,22 @@
         den = jnp.where(some, den, 1.0)
         invs.append(1.0 / den)
         lses.append(jnp.where(some, tops[s] + jnp.log(den), NEG))
+    weights = []
     for r in range(CAP):
         w = jnp.zeros((8, 128), F32)
         for s in range(SLOTS):
             w = jnp.where(mine[r][s], es[r] * invs[s], w)
-        wn_s[r] = w
+        weights.append(w)
+    wide = jnp.concatenate(weights + weights, axis=0).T
+    high = wide.astype(BF16).astype(F32)
+    left128 = iota((nsrc, 128), 1) < 64
+
+    def pairs(x):
+        return jnp.where(left128, x, pltpu.roll(x, nsrc - 1, 0))
+
+    wn_s[0] = pairs(high)
+    wn_s[1] = pairs(wide - high)
+    wn_s[2] = pairs(sg_s[...])
     for d in range(PLANE):
         stat = jnp.full((8, 128), NEG, F32)
         for s in range(SLOTS):
@@ -304,18 +319,13 @@
 
     @pl.loop(0, PLANE)
     def _(d):
-        ws = [pltpu.roll(wn_s[r], (128 - nz * d) % 128, 1) for r in range(CAP)]
         for j in range(nz // 2):
-            scaled = []
-            for a in range(2):
-                for r in range(CAP):
-                    w = jnp.broadcast_to(ws[r][:, 2 * j + a : 2 * j + a + 1], (8, 128))
-                    o = o_s[(d * nz + 2 * j + a) * CAP + r]
-                    scaled.append(jnp.where(w > 0.0, o * w, 0.0))
             i = d * nz + 2 * j
-            sg = jnp.where(lane8[0:1] < 64, sg_s[pl.ds(i, 1), :], sg_s[pl.ds(i + 1, 1), :])
-            pickm = jnp.where(want == sg, 1.0, 0.0).astype(BF16)
-            res = dot_nn(pickm, jnp.concatenate(scaled, axis=0).astype(BF16))
+            o = jnp.concatenate([o_s[i * CAP + k] for k in range(2 * CAP)], axis=0).astype(BF16)
+            hit = want == wn_s[2, pl.ds(i, 1), :]
+            pick = [jnp.where(hit, wn_s[k, pl.ds(i, 1), :], 0.0) for k in range(2)]
+            res = dot_nn(jnp.concatenate(pick, axis=0).astype(BF16), o)
+            res = res[0:64] + res[64:128]
             for a in range(2):
                 even, odd = res[32 * a : 32 * a + 16], res[32 * a + 16 : 32 * a + 32]
                 po_ref[d, 2 * j + a] = jnp.where(left16, pltpu.roll(even, 64, 1), odd).astype(BF16)
@@ -330,8 +340,8 @@
 
 
 def return_kernel(
-    nz, ntp, po_ref, ps_ref, q_hbm, fresh_hbm, w_hbm, resid_hbm, gain_hbm, res_out, norm_out,
-    q_ref, fresh_ref, wv, resid_ref, gain_ref, rc, rsc, ysnd, ystat, ry, rsy, o1, s1, ro2, rs2, parts,
+    nz, ntp, po_ref, ps_ref, q_hbm, fresh_hbm, w_hbm, resid_hbm, res_out, norm_out,
+    q_ref, fresh_ref, wv, resid_ref, rc, rsc, ysnd, ystat, ry, rsy, o1, s1, ro2, rs2, parts,
     in_sem, os_c, or_c, ss_c, sr_c, os_y, or_y, ss_y, sr_y, os_z, or_z, ss_z, sr_z, ts, tr,
 ):
     me, tp = lax.axis_index("req"), lax.axis_index("tp")
@@ -352,7 +362,7 @@
     ins = [
         pltpu.make_async_copy(h, v, in_sem.at[i])
         for i, (h, v) in enumerate(
-            [(q_hbm, q_ref), (fresh_hbm, fresh_ref), (w_hbm, wv), (resid_hbm, resid_ref), (gain_hbm, gain_ref)]
+            [(q_hbm, q_ref), (fresh_hbm, fresh_ref), (w_hbm, wv), (resid_hbm, resid_ref)]
         )
     ]
     start_all(ins)
@@ -488,8 +498,8 @@
         stream = stream + parts[p]
     stream = resid_ref[...].astype(F32) + stream
     mean = jnp.mean(stream * stream, axis=1, keepdims=True)
-    res_out[...] = stream.astype(BF16)
-    norm_out[...] = (stream * lax.rsqrt(mean + 1e-5) * gain_ref[...].astype(F32)).astype(BF16)
+    res_out[...] = stream
+    norm_out[...] = stream * lax.rsqrt(mean + 1e-5)
 
 
 def vmem(n):
@@ -518,9 +528,9 @@
             VM(pool.shape, BF16),
             VM((nsrc * SLOTS, 8, 128), F32),
             VM((nsrc * CAP + 1, 8, 128), F32), VM((nsrc * CAP + 1, 8, 128), F32),
-            VM((CAP, 8, 128), F32),
-            VM((128, 128), F32), VM((128, 128), F32), VM((128, 128), BF16), VM((128, 128), BF16),
-            pltpu.SMEM((56, 128), I32),
+            VM((3, nsrc, 128), F32),
+            VM((UNROLL, 8 * CHUNK, 128), F32), VM((UNROLL, 8 * CHUNK, 128), BF16),
+            pltpu.SMEM((3 * CHUNK + 8, COLUMNS), I32),
             pltpu.SemaphoreType.DMA((2,)),
         ],
         compiler_params=pltpu.CompilerParams(vmem_limit_bytes=24 << 20),
@@ -534,7 +544,7 @@
         functools.partial(dispatch_kernel, nz, npages),
         out_shape=(
             jax.ShapeDtypeStruct((PLANE, nz, 16, 128), BF16),
-            jax.ShapeDtypeStruct((56, 128), I32),
+            jax.ShapeDtypeStruct((3 * CHUNK + 8, COLUMNS), I32),
             jax.ShapeDtypeStruct((16, 128), F32),
             jax.ShapeDtypeStruct((nz * PLANE, 128), F32),
         ),
@@ -557,28 +567,29 @@
     width = o_weight.shape[1]
     DMA = pltpu.SemaphoreType.DMA
     block = (nz, 16, 128)
-    return pl.pallas_call(
+    stream, scaled = pl.pallas_call(
         functools.partial(return_kernel, nz, ntp),
         out_shape=(
-            jax.ShapeDtypeStruct((SLOTS, width), BF16),
-            jax.ShapeDtypeStruct((SLOTS, width), BF16),
+            jax.ShapeDtypeStruct((SLOTS, width), F32),
+            jax.ShapeDtypeStruct((SLOTS, width), F32),
         ),
-        in_specs=vmem(2) + hbm(5),
+        in_specs=vmem(2) + hbm(4),
         out_specs=tuple(vmem(2)),
         scratch_shapes=[
             VM(queries.shape, BF16), VM(fresh_key_value.shape, BF16), VM(o_weight.shape, BF16),
-            VM(resid_in.shape, BF16), VM((1, width), BF16),
+            VM(resid_in.shape, BF16),
             VM((4,) + block, BF16), VM((4, 8, 128), F32), VM((4,) + block, BF16), VM((4, 8, 128), F32),
             VM((3,) + block, BF16), VM((3, 8, 128), F32),
             VM(block, BF16), VM((nz, 1, 128), F32), VM(block, BF16), VM((nz, 1, 128), F32),
             VM((ntp, SLOTS, width), F32),
         ]
-        + [DMA((5,))] + [DMA((4,))] * 4 + [DMA((3,))] * 4 + [DMA((nz - 1,))] * 4 + [DMA((ntp - 1,))] * 2,
+        + [DMA((4,))] + [DMA((4,))] * 4 + [DMA((3,))] * 4 + [DMA((nz - 1,))] * 4 + [DMA((ntp - 1,))] * 2,
         compiler_params=pltpu.CompilerParams(
             collective_id=1, has_side_effects=True, vmem_limit_bytes=12 << 20
         ),
         name="give_back",
-    )(po, ps, *map(in_hbm, (queries, fresh_key_value, o_weight, resid_in, norm_gain.reshape(1, width))))
+    )(po, ps, *map(in_hbm, (queries, fresh_key_value, o_weight, resid_in)))
+    return stream.astype(BF16), (scaled * norm_gain.astype(F32)).astype(BF16)
 
 
 def body(nz, ntp, queries, fresh_key_value, pool, block_owner, block_page, lengths, o_weight, resid_in, norm_gain):

time: 78.6 us -> 73 us (0.929)
  the two profiles are of different devices: /device:TPU:1 before, /device:TPU:8 now
where the time goes in v4:
time: 73 us; the launch traced here: 72.8 us
  Pallas kernels  70.9 us (97%)
  other arithmetic  1.23 us (2%)
    pallas_call x1, Pallas kernels, dispatch_call(): pl.pallas_call(functools.partial(dispatch_kernel, nz, npages), out_shape=...  29.5 us
    pallas_call x1, Pallas kernels, return_call(): pl.pallas_call(functools.partial(return_kernel, nz, ntp), out_shape=(jax....  29 us
    pallas_call x1, Pallas kernels, owner_call(): pl.pallas_call(functools.partial(owner_kernel, nz), out_shape=(jax.ShapeD...  12.4 us

profile of v4, /device:TPU:8, one launch (start us, length us, event | category | flops | bytes accessed | tf_op | source)
XLA Modules:
  0.0 72.8 jit_solution(824891803678267350)
XLA Ops:
  0.6 29.5 %dispatch.1 = (bf16[8,16,16,128]{3,2,1,0:T(8,128)(2,1)S(1)}, s32[56,128]{1,0:T(8,128)S(1)}, f32[16,128]{1,0:T(8,128)S(1)}, f32[128,128]{1,0:T(8,128)S(1)}) custom-call(bf16[4,512]{1,0:T(4,128)(2,1)} %q_hbm.3, s32[4,128]{1,0:T(4,128)} %bitcast.2, s32[4,128]{1,0:T(4,128)} %bitcast.3, s32[4]{0:T(128)} %len_hbm.1), custom_call_target="tpu_custom_call" | custom-call | tf_op jit(solution)/shard_map/dispatch/pallas_call | solution.py:543
  30.2 0.0 copy-start
  30.2 12.4 %owner.1 = (bf16[8,16,16,128]{3,2,1,0:T(8,128)(2,1)S(1)}, f32[8,8,128]{2,1,0:T(8,128)S(1)}) custom-call(bf16[8,16,16,128]{3,2,1,0:T(8,128)(2,1)S(1)} %get-tuple-element.10.qall_ref, s32[56,128]{1,0:T(8,128)S(1)} %get-tuple-element.11.lists_ref, f32[16,128]{1,0:T(8,128)S(1)} %get-tuple-element.12.items_ref, f32[128,128]{1,0:T(8,128)S(1)} %get-tuple-element.13.sg_s, ...), custom_call_target="tpu_custom_call" | custom-call | tf_op jit(solution)/shard_map/owner/pallas_call | solution.py:519
  42.6 29.0 %give_back.1 = (f32[4,2048]{1,0:T(4,128)S(1)}, f32[4,2048]{1,0:T(4,128)S(1)}) custom-call(bf16[8,16,16,128]{3,2,1,0:T(8,128)(2,1)S(1)} %get-tuple-element.14.po_ref, f32[8,8,128]{2,1,0:T(8,128)S(1)} %get-tuple-element.15.ps_ref, bf16[4,512]{1,0:T(4,128)(2,1)} %q_hbm.3, bf16[4,128]{1,0:T(4,128)(2,1)} %fresh_hbm.1, bf16[512,2048]{1,0:T(8,128)(2,1)} %w_hbm.1, ...), custom_call_target="tpu_custom_call" | custom-call | tf_op jit(solution)/shard_map/give_back/pallas_call | solution.py:570
  71.6 0.0 copy-done
  71.6 0.6 multiply_convert_fusion
  72.2 0.6 convert_element_type.9
  (1 shorter events, 0.0 us)
Async XLA Ops:
  30.2 41.4 %copy-start = (bf16[2048]{0:T(1024)(128)(2,1)S(1)}, bf16[2048]{0:T(1024)(128)(2,1)}, u32[]{:S(2)}) copy-start(bf16[2048]{0:T(1024)(128)(2,1)} %param.17) | copy-start | bytes 12292

commit v5 on v4

--- a/solution.py
+++ b/solution.py
@@ -123,52 +123,68 @@
     ]
     start_all(ins)
     ins[0].wait()
-    zq[z] = head_pair_rows(q_v[...].astype(F32)).astype(BF16)
+    zq[z % 2, z // 2] = head_pair_rows(q_v[...].astype(F32)).astype(BF16)
     pl.semaphore_wait(barrier, nz - 1 + PLANE - 1)
+    mine = zq.at[z % 2, z // 2]
     q_z = [
-        remote(zq.at[z], zq.at[z], qs_z.at[i], qr_z.at[i], {"req": p * PLANE + yc}) for i, p in enumerate(zpeers)
+        [
+            remote(mine, mine, qs_z.at[k - 1], qr_z.at[k - 1], {"req": (z + k) % nz * PLANE + yc})
+            for k in far_first(nz)
+            if k % 2 == h
+        ]
+        for h in range(2)
     ]
-    start_all(q_z)
+    start_all(q_z[0] + q_z[1])
 
     wait_all(ins[1:])
     rows, lanes = iota((128, 128), 0), iota((128, 128), 1)
     tri = jnp.where(rows <= lanes, 1.0, 0.0).astype(BF16)
     ones = jnp.ones((128, 128), BF16)
     base = jnp.zeros((128, 128), F32)
-    table = jnp.zeros((128, 128), F32)
+    table = jnp.zeros((32, 128), F32)
     for s in range(SLOTS):
         live = jnp.clip(len_s[s] - iota((1, 128), 1) * 128, 0, 128)
         hit = jnp.logical_and(rows == owner_v[s : s + 1, :], live > 0)
         hot = jnp.where(hit, 1.0, 0.0).astype(BF16)
         rank = jnp.sum(jnp.where(hit, base + dot_nn(hot, tri) - 1.0, 0.0), axis=0, keepdims=True)
         base = base + dot_nn(hot, ones)
-        kind = rows // CAP
+        kind = rows % 32 // CAP
+        quarter = rows // 32 == owner_v[s : s + 1, :] % 4
         val = jnp.where(
             kind == 0, page_v[s : s + 1, :].astype(F32),
             jnp.where(kind == 1, live.astype(F32), jnp.where(kind == 2, float(s), 0.0)),
         )
-        place = jnp.where((rows % CAP).astype(F32) == rank, val, 0.0).astype(BF16)
-        table = table + dot_nt(hot, place)
-    zsend[...] = table.reshape(nz, PLANE, 128).astype(BF16)
+        place = jnp.where(jnp.logical_and(quarter, (rows % CAP).astype(F32) == rank), val, 0.0).astype(BF16)
+        four = jnp.logical_and(rows[0:32] == owner_v[s : s + 1, :] // 4, live > 0)
+        table = table + dot_nt(jnp.where(four, 1.0, 0.0).astype(BF16), place)
+    for i in range(nz):
+        zsend[i] = table[2 * i : 2 * i + 2].astype(BF16)
     zm[z] = zsend[z]
     m_z = [
         remote(zsend.at[p], zm.at[z], ms_z.at[i], mr_z.at[i], {"req": p * PLANE + yc}) for i, p in enumerate(zpeers)
     ]
     start_all(m_z)
 
-    wait_all(q_z)
-    q_y = [
-        remote(zq, qall_ref.at[yc], qs_y.at[i], qr_y.at[i], {"req": z * PLANE + 2 * p + core})
-        for i, p in enumerate(ypeers)
-    ]
-    q_c = [remote(zq, qall_ref.at[yc], qs_c.at[3], qr_c.at[3], {"req": z * PLANE + sib})]
-    start_all(q_y + q_c)
+    q_y, q_c = [], []
+    for h in range(2):
+        wait_all(q_z[h])
+        part = (z + h) % 2
+        for i, p in enumerate(ypeers):
+            to = {"req": z * PLANE + 2 * p + core}
+            q_y.append(remote(zq.at[part], qall_ref.at[yc, part], qs_y.at[3 * h + i], qr_y.at[3 * h + i], to))
+        q_c.append(
+            remote(zq.at[part], qall_ref.at[yc, part], qs_c.at[6 + h], qr_c.at[6 + h], {"req": z * PLANE + sib})
+        )
+        start_all(q_y[-3:] + q_c[-1:])
     qall_ref[yc] = zq[...]
 
     wait_all(m_z)
-    got = zm[...].astype(F32)
+    got = [zm[i].astype(F32) for i in range(nz)]
     for d in range(PLANE):
-        ysend[d] = jnp.concatenate([got[i, d : d + 1, :] for i in range(nz)], axis=0).astype(BF16)
+        half = jnp.concatenate([g[d // 4 : d // 4 + 1, :] for g in got], axis=0)
+        if d % 4:
+            half = pltpu.roll(half, 128 - 32 * (d % 4), 1)
+        ysend[d] = half.astype(BF16)
     mall[yc] = ysend[yc]
     m_y = [
         remote(ysend.at[p], mall.at[yc], ms_y.at[i], mr_y.at[i], {"req": z * PLANE + p}) for i, p in enumerate(plane)
@@ -176,12 +192,13 @@
     start_all(m_y)
     wait_all(m_y)
     sort_items(nz * PLANE, npages, mall[...].reshape(nz * PLANE, 128), lists_ref, items_ref, slots_ref)
-    for i, p in enumerate((2, 3, 1)):
-        q_y[i].wait()
-        slot = (y + p) % 4 * 2 + core
-        c = remote(qall_ref.at[slot], qall_ref.at[slot], qs_c.at[i], qr_c.at[i], {"req": z * PLANE + sib})
-        c.start()
-        q_c.append(c)
+    for h in range(2):
+        for i, p in enumerate((2, 3, 1)):
+            q_y[3 * h + i].wait()
+            here = qall_ref.at[(y + p) % 4 * 2 + core, (z + h) % 2]
+            c = remote(here, here, qs_c.at[3 * h + i], qr_c.at[3 * h + i], {"req": z * PLANE + sib})
+            c.start()
+            q_c.append(c)
     wait_all(q_c)
 
 
@@ -205,7 +222,7 @@
     def _(g):
         for u in range(group):
             i = g * group + u
-            q = qall_ref[i // nz, i % nz].astype(F32)
+            q = qall_ref[i // nz, i % 2, i % nz // 2].astype(F32)
             for r in range(CAP):
                 o_s[i * CAP + r] = jnp.zeros((8, 128), F32)
             for t in range(2):
@@ -395,69 +412,86 @@
         self_score.append(jnp.where(left, ls, rsum) * 0.125)
         self_value.append(jnp.where(left, other, kv))
 
-    ys = []
-    for i, p in enumerate(yorder):
-        wait_all(cores[i])
-        ours = 2 * p + core
-        sa, sb = ps_ref[ours], rsc[i]
-        top = jnp.maximum(sa, sb)
-        ea, eb = jnp.exp(sa - top), jnp.exp(sb - top)
-        both = ea + eb
-        ystat[i] = top + jnp.log(both)
-        yl, yr = spread_weights(ea / both, nz)
-        for zi in range(nz):
+    def from_here(x):
+        ahead = pltpu.roll(x, (128 - z) % 128, 1)
+        behind = pltpu.roll(x, nz - z, 1)
+        return jnp.where(lane8 % nz + z < nz, ahead, behind)
+
+    ys = [[], []]
+    sides, stats = [], []
+    for h in range(2):
+        for i, p in enumerate(yorder):
+            ours = 2 * p + core
+            if h == 0:
+                wait_all(cores[i])
+                sa, sb = ps_ref[ours], rsc[i]
+                top = jnp.maximum(sa, sb)
+                ea, eb = jnp.exp(sa - top), jnp.exp(sb - top)
+                both = ea + eb
+                ystat[i] = from_here(top + jnp.log(both))
+                sides.append(spread_weights(from_here(ea / both), nz))
+            yl, yr = sides[i]
+            for j in range(nz // 2):
+                k = 2 * j + h
+                halves = []
+                zi = (z + k) % nz
+                pa, pb = po_ref[ours, zi].astype(F32), rc[i, zi].astype(F32)
+                for t in range(2):
+                    li = 2 * t * nz + k
+                    w = jnp.where(left, yl[:, li : li + 1], yr[:, li : li + 1])
+                    b = pb[8 * t : 8 * t + 8]
+                    halves.append(b + w * (pa[8 * t : 8 * t + 8] - b))
+                ysnd[i, h, j] = jnp.concatenate(halves, axis=0).astype(BF16)
+            if i < 3:
+                to = {"req": z * PLANE + 2 * p + core}
+                if h == 0:
+                    ys[h].append(remote(ystat.at[i], rsy.at[i], ss_y.at[i], sr_y.at[i], to))
+                    ys[h][-1].start()
+                ys[h].append(
+                    remote(ysnd.at[i, h], ry.at[i, h], os_y.at[3 * h + i], or_y.at[3 * h + i], to)
+                )
+                ys[h][-1].start()
+
+    zs = []
+    for h in range(2):
+        wait_all(ys[h])
+        if h == 0:
+            stats = [rsy[p] for p in range(3)] + [ystat[3]]
+            top = stats[0]
+            for p in range(1, 4):
+                top = jnp.maximum(top, stats[p])
+            ws = [jnp.exp(s - top) for s in stats]
+            wsum = ws[0]
+            for p in range(1, 4):
+                wsum = wsum + ws[p]
+            lse = top + jnp.log(wsum)
+            sides = [spread_weights(w / wsum, nz) for w in ws]
+            by_slot = [pltpu.roll(lse, (128 - nz * s) % 128, 1) if s else lse for s in range(SLOTS)]
+            rows = jnp.concatenate(by_slot + [jnp.zeros((96, 128), F32)], axis=0).T
+            for k in range(nz):
+                s1[k] = rows[k : k + 1]
+        for j in range(nz // 2):
+            k = 2 * j + h
+            pieces = [ry[p, h, j].astype(F32) for p in range(3)] + [ysnd[3, h, j].astype(F32)]
             halves = []
-            pa, pb = po_ref[ours, zi].astype(F32), rc[i, zi].astype(F32)
             for t in range(2):
-                li = 2 * t * nz + zi
-                w = jnp.where(left, yl[:, li : li + 1], yr[:, li : li + 1])
-                b = pb[8 * t : 8 * t + 8]
-                halves.append(b + w * (pa[8 * t : 8 * t + 8] - b))
-            ysnd[i, zi] = jnp.concatenate(halves, axis=0).astype(BF16)
-        if i < 3:
-            to = {"req": z * PLANE + 2 * p + core}
-            ys.append(remote(ystat.at[i], rsy.at[i], ss_y.at[i], sr_y.at[i], to))
-            ys.append(remote(ysnd.at[i], ry.at[i], os_y.at[i], or_y.at[i], to))
-            start_all(ys[-2:])
-    wait_all(ys)
-
-    stats = [rsy[p] for p in range(3)] + [ystat[3]]
-    top = stats[0]
-    for p in range(1, 4):
-        top = jnp.maximum(top, stats[p])
-    ws = [jnp.exp(s - top) for s in stats]
-    wsum = ws[0]
-    for p in range(1, 4):
-        wsum = wsum + ws[p]
-    lse = top + jnp.log(wsum)
-    sides = [spread_weights(w / wsum, nz) for w in ws]
-    for zi in range(nz):
-        pieces = [ry[p, zi].astype(F32) for p in range(3)] + [ysnd[3, zi].astype(F32)]
-        halves = []
-        for t in range(2):
-            li = 2 * t * nz + zi
-            total = jnp.zeros((8, 128), F32)
-            for p in range(4):
-                yl, yr = sides[p]
-                w = jnp.where(left, yl[:, li : li + 1], yr[:, li : li + 1])
-                total = total + w * pieces[p][8 * t : 8 * t + 8]
-            halves.append(total)
-        o1[zi] = jnp.concatenate(halves, axis=0).astype(BF16)
-    by_slot = [pltpu.roll(lse, (128 - nz * s) % 128, 1) if s else lse for s in range(SLOTS)]
-    rows = jnp.concatenate(by_slot + [jnp.zeros((96, 128), F32)], axis=0).T
-    for zi in range(nz):
-        s1[zi] = rows[zi : zi + 1]
-    ro2[z] = o1[z]
-    rs2[z] = s1[z]
-    copies = []
-    for i, p in enumerate(zpeers):
-        to = {"req": p * PLANE + yc}
-        copies.append(remote(o1.at[p], ro2.at[z], os_z.at[i], or_z.at[i], to))
-        copies.append(remote(s1.at[p], rs2.at[z], ss_z.at[i], sr_z.at[i], to))
-    for c in copies:
-        c.start()
-    for c in copies:
-        c.wait()
+                li = 2 * t * nz + k
+                total = jnp.zeros((8, 128), F32)
+                for p in range(4):
+                    yl, yr = sides[p]
+                    w = jnp.where(left, yl[:, li : li + 1], yr[:, li : li + 1])
+                    total = total + w * pieces[p][8 * t : 8 * t + 8]
+                halves.append(total)
+            o1[k] = jnp.concatenate(halves, axis=0).astype(BF16)
+        for k in far_first(nz):
+            if k % 2 == h:
+                to = {"req": (z + k) % nz * PLANE + yc}
+                zs.append(remote(s1.at[k], rs2.at[z], ss_z.at[k - 1], sr_z.at[k - 1], to))
+                zs.append(remote(o1.at[k], ro2.at[z], os_z.at[k - 1], or_z.at[k - 1], to))
+                start_all(zs[-2:])
+    ro2[z] = o1[0]
+    rs2[z] = s1[0]
+    wait_all(zs)
 
     st = jnp.concatenate([rs2[zi] for zi in range(nz)], axis=0)
     top = jnp.max(st, axis=0, keepdims=True)
@@ -543,7 +577,7 @@
     return pl.pallas_call(
         functools.partial(dispatch_kernel, nz, npages),
         out_shape=(
-            jax.ShapeDtypeStruct((PLANE, nz, 16, 128), BF16),
+            jax.ShapeDtypeStruct((PLANE, 2, nz // 2, 16, 128), BF16),
             jax.ShapeDtypeStruct((3 * CHUNK + 8, COLUMNS), I32),
             jax.ShapeDtypeStruct((16, 128), F32),
             jax.ShapeDtypeStruct((nz * PLANE, 128), F32),
@@ -552,10 +586,10 @@
         out_specs=tuple(vmem(4)),
         scratch_shapes=[
             VM(queries.shape, BF16), VM((SLOTS, 128), I32), VM((SLOTS, 128), I32), pltpu.SMEM((SLOTS,), I32),
-            VM((nz, 16, 128), BF16), VM((nz, PLANE, 128), BF16), VM((nz, PLANE, 128), BF16),
+            VM((2, nz // 2, 16, 128), BF16), VM((nz, 2, 128), BF16), VM((nz, 2, 128), BF16),
             VM((PLANE, nz, 128), BF16), VM((PLANE, nz, 128), BF16),
         ]
-        + [DMA((4,))] + [DMA((nz - 1,))] * 4 + [DMA((3,))] * 2 + [DMA((4,))] * 2 + [DMA((PLANE - 1,))] * 2,
+        + [DMA((4,))] + [DMA((nz - 1,))] * 4 + [DMA((6,))] * 2 + [DMA((8,))] * 2 + [DMA((PLANE - 1,))] * 2,
         compiler_params=pltpu.CompilerParams(
             collective_id=0, has_side_effects=True, vmem_limit_bytes=6 << 20
         ),
@@ -566,7 +600,7 @@
 def return_call(nz, ntp, po, ps, queries, fresh_key_value, o_weight, resid_in, norm_gain):
     width = o_weight.shape[1]
     DMA = pltpu.SemaphoreType.DMA
-    block = (nz, 16, 128)
+    block, half = (nz, 16, 128), (2, nz // 2, 16, 128)
     stream, scaled = pl.pallas_call(
         functools.partial(return_kernel, nz, ntp),
         out_shape=(
@@ -578,12 +612,12 @@
         scratch_shapes=[
             VM(queries.shape, BF16), VM(fresh_key_value.shape, BF16), VM(o_weight.shape, BF16),
             VM(resid_in.shape, BF16),
-            VM((4,) + block, BF16), VM((4, 8, 128), F32), VM((4,) + block, BF16), VM((4, 8, 128), F32),
-            VM((3,) + block, BF16), VM((3, 8, 128), F32),
+            VM((4,) + block, BF16), VM((4, 8, 128), F32), VM((4,) + half, BF16), VM((4, 8, 128), F32),
+            VM((3,) + half, BF16), VM((3, 8, 128), F32),
             VM(block, BF16), VM((nz, 1, 128), F32), VM(block, BF16), VM((nz, 1, 128), F32),
             VM((ntp, SLOTS, width), F32),
         ]
-        + [DMA((4,))] + [DMA((4,))] * 4 + [DMA((3,))] * 4 + [DMA((nz - 1,))] * 4 + [DMA((ntp - 1,))] * 2,
+        + [DMA((4,))] + [DMA((4,))] * 4 + [DMA((6,))] * 2 + [DMA((3,))] * 2 + [DMA((nz - 1,))] * 4 + [DMA((ntp - 1,))] * 2,
         compiler_params=pltpu.CompilerParams(
             collective_id=1, has_side_effects=True, vmem_limit_bytes=12 << 20
         ),

time: 73 us -> 72.5 us (level)
  the two profiles are of different devices: /device:TPU:8 before, /device:TPU:1 now
where the time goes in v5:
time: 72.5 us; the launch traced here: 72 us
  Pallas kernels  70.1 us (97%)
  other arithmetic  1.23 us (2%)
    pallas_call x1, Pallas kernels, dispatch_call(): pl.pallas_call(functools.partial(dispatch_kernel, nz, npages), out_shape=...  31.4 us
    pallas_call x1, Pallas kernels, return_call(): pl.pallas_call(functools.partial(return_kernel, nz, ntp), out_shape=(jax....  25.8 us
    pallas_call x1, Pallas kernels, owner_call(): pl.pallas_call(functools.partial(owner_kernel, nz), out_shape=(jax.ShapeD...  12.9 us

profile of v5, /device:TPU:1, one launch (start us, length us, event | category | flops | bytes accessed | tf_op | source)
XLA Modules:
  0.0 72.0 jit_solution(1755603763621293867)
XLA Ops:
  0.6 31.4 %dispatch.1 = (bf16[8,2,8,16,128]{4,3,2,1,0:T(8,128)(2,1)S(1)}, s32[56,128]{1,0:T(8,128)S(1)}, f32[16,128]{1,0:T(8,128)S(1)}, f32[128,128]{1,0:T(8,128)S(1)}) custom-call(bf16[4,512]{1,0:T(4,128)(2,1)} %q_hbm.3, s32[4,128]{1,0:T(4,128)} %bitcast.2, s32[4,128]{1,0:T(4,128)} %bitcast.3, s32[4]{0:T(128)} %len_hbm.1), custom_call_target="tpu_custom_call" | custom-call | tf_op jit(solution)/shard_map/dispatch/pallas_call | solution.py:577
  32.0 0.0 copy-start
  32.0 12.9 %owner.1 = (bf16[8,16,16,128]{3,2,1,0:T(8,128)(2,1)S(1)}, f32[8,8,128]{2,1,0:T(8,128)S(1)}) custom-call(bf16[8,2,8,16,128]{4,3,2,1,0:T(8,128)(2,1)S(1)} %get-tuple-element.10.qall_ref, s32[56,128]{1,0:T(8,128)S(1)} %get-tuple-element.11.lists_ref, f32[16,128]{1,0:T(8,128)S(1)} %get-tuple-element.12.items_ref, f32[128,128]{1,0:T(8,128)S(1)} %get-tuple-element.13.sg_s, ...), custom_call_target="tpu_custom_call" | custom-call | tf_op jit(solution)/shard_map/owner/pallas_call | solution.py:553
  45.0 25.8 %give_back.1 = (f32[4,2048]{1,0:T(4,128)S(1)}, f32[4,2048]{1,0:T(4,128)S(1)}) custom-call(bf16[8,16,16,128]{3,2,1,0:T(8,128)(2,1)S(1)} %get-tuple-element.14.po_ref, f32[8,8,128]{2,1,0:T(8,128)S(1)} %get-tuple-element.15.ps_ref, bf16[4,512]{1,0:T(4,128)(2,1)} %q_hbm.3, bf16[4,128]{1,0:T(4,128)(2,1)} %fresh_hbm.1, bf16[512,2048]{1,0:T(8,128)(2,1)} %w_hbm.1, ...), custom_call_target="tpu_custom_call" | custom-call | tf_op jit(solution)/shard_map/give_back/pallas_call | solution.py:604
  70.7 0.0 copy-done
  70.8 0.6 multiply_convert_fusion
  71.4 0.6 convert_element_type.9
  (1 shorter events, 0.0 us)
Async XLA Ops:
  32.0 38.7 %copy-start = (bf16[2048]{0:T(1024)(128)(2,1)S(1)}, bf16[2048]{0:T(1024)(128)(2,1)}, u32[]{:S(2)}) copy-start(bf16[2048]{0:T(1024)(128)(2,1)} %param.17) | copy-start | bytes 12292

commit v6 on v5

--- a/solution.py
+++ b/solution.py
@@ -111,7 +111,6 @@
     sib = yc + 1 - 2 * core
     zpeers = [(z + k) % nz for k in far_first(nz)]
     plane = [(yc + k) % PLANE for k in range(1, PLANE)]
-    ypeers = [(y + k) % 4 for k in (2, 1, 3)]
     barrier = pltpu.get_barrier_semaphore()
     for p in zpeers:
         pl.semaphore_signal(barrier, inc=1, device_id={"req": p * PLANE + yc}, device_id_type=MESH)
@@ -165,18 +164,33 @@
     ]
     start_all(m_z)
 
-    q_y, q_c = [], []
+    def over_y(k, src, sem):
+        to = {"req": z * PLANE + (y + k) % 4 * 2 + core}
+        return lambda dst: remote(src, dst, qs_y.at[sem], qr_y.at[sem], to)
+
+    def cross(ref, sem):
+        c = remote(ref, ref, qs_c.at[sem], qr_c.at[sem], {"req": z * PLANE + sib})
+        c.start()
+        q_c.append(c)
+
+    def from_y(k, h):
+        return qall_ref.at[(y + k) % 4 * 2 + core, (z + h) % 2]
+
+    q_up, q_down, q_c = [], [], []
     for h in range(2):
         wait_all(q_z[h])
         part = (z + h) % 2
-        for i, p in enumerate(ypeers):
-            to = {"req": z * PLANE + 2 * p + core}
-            q_y.append(remote(zq.at[part], qall_ref.at[yc, part], qs_y.at[3 * h + i], qr_y.at[3 * h + i], to))
-        q_c.append(
-            remote(zq.at[part], qall_ref.at[yc, part], qs_c.at[6 + h], qr_c.at[6 + h], {"req": z * PLANE + sib})
-        )
-        start_all(q_y[-3:] + q_c[-1:])
+        q_up.append(over_y(1, zq.at[part], 2 * h)(from_y(0, h)))
+        q_down.append(over_y(3, zq.at[part], 2 * h + 1)(from_y(0, h)))
+        start_all([q_up[h], q_down[h]])
+        c = remote(zq.at[part], from_y(0, h), qs_c.at[6 + h], qr_c.at[6 + h], {"req": z * PLANE + sib})
+        c.start()
+        q_c.append(c)
     qall_ref[yc] = zq[...]
+    q_up[0].wait()
+    relay = [over_y(1, from_y(3, 0), 4)(from_y(3, 0))]
+    relay[0].start()
+    cross(from_y(3, 0), 0)
 
     wait_all(m_z)
     got = [zm[i].astype(F32) for i in range(nz)]
@@ -190,15 +204,19 @@
         remote(ysend.at[p], mall.at[yc], ms_y.at[i], mr_y.at[i], {"req": z * PLANE + p}) for i, p in enumerate(plane)
     ]
     start_all(m_y)
+    q_down[1].wait()
+    relay.append(over_y(3, from_y(1, 1), 5)(from_y(1, 1)))
+    relay[1].start()
+    cross(from_y(1, 1), 1)
     wait_all(m_y)
     sort_items(nz * PLANE, npages, mall[...].reshape(nz * PLANE, 128), lists_ref, items_ref, slots_ref)
+    q_down[0].wait()
+    cross(from_y(1, 0), 2)
+    q_up[1].wait()
+    cross(from_y(3, 1), 3)
     for h in range(2):
-        for i, p in enumerate((2, 3, 1)):
-            q_y[3 * h + i].wait()
-            here = qall_ref.at[(y + p) % 4 * 2 + core, (z + h) % 2]
-            c = remote(here, here, qs_c.at[3 * h + i], qr_c.at[3 * h + i], {"req": z * PLANE + sib})
-            c.start()
-            q_c.append(c)
+        relay[h].wait()
+        cross(from_y(2, h), 4 + h)
     wait_all(q_c)
 
 
@@ -216,13 +234,12 @@
     live, slot = items_ref[0:8], items_ref[8:16]
 
     keep = jnp.where(left, 0.125, 0.0)
-    group = 8
-
-    @pl.loop(0, nsrc // group)
+
+    @pl.loop(0, 2 * PLANE)
     def _(g):
-        for u in range(group):
-            i = g * group + u
-            q = qall_ref[i // nz, i % 2, i % nz // 2].astype(F32)
+        for j in range(nz // 2):
+            i = g // 2 * nz + 2 * j + g % 2
+            q = qall_ref[g // 2, g % 2, j].astype(F32)
             for r in range(CAP):
                 o_s[i * CAP + r] = jnp.zeros((8, 128), F32)
             for t in range(2):
@@ -519,7 +536,7 @@
     sel = jnp.where(iota((16, 16), 1) // 4 == iota((16, 16), 0), 1.0, 0.0).astype(BF16)
     lhs = dot_nn(sel, wide).astype(BF16)
     wait_all(ins[2:])
-    parts[tp] = dot_nn(lhs, wv[...])[0:SLOTS]
+    parts[tp] = dot_nn(lhs, wv[...])[0:SLOTS].astype(BF16)
     copies = []
     for i, p in enumerate(tpeers):
         copies.append(remote(parts.at[tp], parts.at[tp], ts.at[i], tr.at[i], {"tp": p}))
@@ -527,9 +544,9 @@
         c.start()
     for c in copies:
         c.wait()
-    stream = parts[0]
+    stream = parts[0].astype(F32)
     for p in range(1, ntp):
-        stream = stream + parts[p]
+        stream = stream + parts[p].astype(F32)
     stream = resid_ref[...].astype(F32) + stream
     mean = jnp.mean(stream * stream, axis=1, keepdims=True)
     res_out[...] = stream
@@ -615,7 +632,7 @@
             VM((4,) + block, BF16), VM((4, 8, 128), F32), VM((4,) + half, BF16), VM((4, 8, 128), F32),
             VM((3,) + half, BF16), VM((3, 8, 128), F32),
             VM(block, BF16), VM((nz, 1, 128), F32), VM(block, BF16), VM((nz, 1, 128), F32),
-            VM((ntp, SLOTS, width), F32),
+            VM((ntp, SLOTS, width), BF16),
         ]
         + [DMA((4,))] + [DMA((4,))] * 4 + [DMA((6,))] * 2 + [DMA((3,))] * 2 + [DMA((nz - 1,))] * 4 + [DMA((ntp - 1,))] * 2,
         compiler_params=pltpu.CompilerParams(

time: 72.5 us -> 73.4 us (1.012); the launches traced: 72 us -> 72.1 us
    pallas_call x1, Pallas kernels: 12.9 us -> 11.9 us  [owner_call(): pl.pallas_call(functools.partial(owner_kernel, nz), out_shape=(jax.ShapeD...]
    pallas_call x1, Pallas kernels: 31.4 us -> 32.2 us  [dispatch_call(): pl.pallas_call(functools.partial(dispatch_kernel, nz, npages), out_shape=...]
where the time goes in v6:
time: 73.4 us; the launch traced here: 72.1 us
  Pallas kernels  70.2 us (96%)
  other arithmetic  1.23 us (2%)
    pallas_call x1, Pallas kernels, dispatch_call(): pl.pallas_call(functools.partial(dispatch_kernel, nz, npages), out_shape=...  32.2 us
    pallas_call x1, Pallas kernels, return_call(): pl.pallas_call(functools.partial(return_kernel, nz, ntp), out_shape=(jax....  26.1 us
    pallas_call x1, Pallas kernels, owner_call(): pl.pallas_call(functools.partial(owner_kernel, nz), out_shape=(jax.ShapeD...  11.9 us

profile of v6, /device:TPU:1, one launch (start us, length us, event | category | flops | bytes accessed | tf_op | source)
XLA Modules:
  0.0 72.1 jit_solution(12477642956725010886)
XLA Ops:
  0.6 32.2 %dispatch.1 = (bf16[8,2,8,16,128]{4,3,2,1,0:T(8,128)(2,1)S(1)}, s32[56,128]{1,0:T(8,128)S(1)}, f32[16,128]{1,0:T(8,128)S(1)}, f32[128,128]{1,0:T(8,128)S(1)}) custom-call(bf16[4,512]{1,0:T(4,128)(2,1)} %q_hbm.3, s32[4,128]{1,0:T(4,128)} %bitcast.2, s32[4,128]{1,0:T(4,128)} %bitcast.3, s32[4]{0:T(128)} %len_hbm.1), custom_call_target="tpu_custom_call" | custom-call | tf_op jit(solution)/shard_map/dispatch/pallas_call | solution.py:594
  32.8 0.0 copy-start
  32.8 11.9 %owner.1 = (bf16[8,16,16,128]{3,2,1,0:T(8,128)(2,1)S(1)}, f32[8,8,128]{2,1,0:T(8,128)S(1)}) custom-call(bf16[8,2,8,16,128]{4,3,2,1,0:T(8,128)(2,1)S(1)} %get-tuple-element.10.qall_ref, s32[56,128]{1,0:T(8,128)S(1)} %get-tuple-element.11.lists_ref, f32[16,128]{1,0:T(8,128)S(1)} %get-tuple-element.12.items_ref, f32[128,128]{1,0:T(8,128)S(1)} %get-tuple-element.13.sg_s, ...), custom_call_target="tpu_custom_call" | custom-call | tf_op jit(solution)/shard_map/owner/pallas_call | solution.py:570
  44.8 26.1 %give_back.1 = (f32[4,2048]{1,0:T(4,128)S(1)}, f32[4,2048]{1,0:T(4,128)S(1)}) custom-call(bf16[8,16,16,128]{3,2,1,0:T(8,128)(2,1)S(1)} %get-tuple-element.14.po_ref, f32[8,8,128]{2,1,0:T(8,128)S(1)} %get-tuple-element.15.ps_ref, bf16[4,512]{1,0:T(4,128)(2,1)} %q_hbm.3, bf16[4,128]{1,0:T(4,128)(2,1)} %fresh_hbm.1, bf16[512,2048]{1,0:T(8,128)(2,1)} %w_hbm.1, ...), custom_call_target="tpu_custom_call" | custom-call | tf_op jit(solution)/shard_map/give_back/pallas_call | solution.py:621
  70.9 0.0 copy-done
  70.9 0.6 multiply_convert_fusion
  71.5 0.6 convert_element_type.9
  (1 shorter events, 0.0 us)
Async XLA Ops:
  32.8 38.0 %copy-start = (bf16[2048]{0:T(1024)(128)(2,1)S(1)}, bf16[2048]{0:T(1024)(128)(2,1)}, u32[]{:S(2)}) copy-start(bf16[2048]{0:T(1024)(128)(2,1)} %param.17) | copy-start | bytes 12292

commit v7 on v5

--- a/solution.py
+++ b/solution.py
@@ -216,13 +216,12 @@
     live, slot = items_ref[0:8], items_ref[8:16]
 
     keep = jnp.where(left, 0.125, 0.0)
-    group = 8
-
-    @pl.loop(0, nsrc // group)
+
+    @pl.loop(0, 2 * PLANE)
     def _(g):
-        for u in range(group):
-            i = g * group + u
-            q = qall_ref[i // nz, i % 2, i % nz // 2].astype(F32)
+        for j in range(nz // 2):
+            i = g // 2 * nz + 2 * j + g % 2
+            q = qall_ref[g // 2, g % 2, j].astype(F32)
             for r in range(CAP):
                 o_s[i * CAP + r] = jnp.zeros((8, 128), F32)
             for t in range(2):
@@ -533,7 +532,7 @@
     stream = resid_ref[...].astype(F32) + stream
     mean = jnp.mean(stream * stream, axis=1, keepdims=True)
     res_out[...] = stream
-    norm_out[...] = stream * lax.rsqrt(mean + 1e-5)
+    norm_out[...] = jnp.broadcast_to(lax.rsqrt(mean + 1e-5), stream.shape)
 
 
 def vmem(n):
@@ -601,7 +600,7 @@
     width = o_weight.shape[1]
     DMA = pltpu.SemaphoreType.DMA
     block, half = (nz, 16, 128), (2, nz // 2, 16, 128)
-    stream, scaled = pl.pallas_call(
+    stream, scale = pl.pallas_call(
         functools.partial(return_kernel, nz, ntp),
         out_shape=(
             jax.ShapeDtypeStruct((SLOTS, width), F32),
@@ -623,7 +622,7 @@
         ),
         name="give_back",
     )(po, ps, *map(in_hbm, (queries, fresh_key_value, o_weight, resid_in)))
-    return stream.astype(BF16), (scaled * norm_gain.astype(F32)).astype(BF16)
+    return stream.astype(BF16), (stream * scale * norm_gain.astype(F32)).astype(BF16)
 
 
 def body(nz, ntp, queries, fresh_key_value, pool, block_owner, block_page, lengths, o_weight, resid_in, norm_gain):

time: 72.5 us -> 70.5 us (0.972)
  Pallas kernels: 70.1 us -> 68.7 us
    pallas_call x1, Pallas kernels: 12.9 us -> 11.9 us  [owner_call(): pl.pallas_call(functools.partial(owner_kernel, nz), out_shape=(jax.ShapeD...]
where the time goes in v7:
time: 70.5 us; the launch traced here: 70 us
  Pallas kernels  68.7 us (97%)
    pallas_call x1, Pallas kernels, dispatch_call(): pl.pallas_call(functools.partial(dispatch_kernel, nz, npages), out_shape=...  31.4 us
    pallas_call x1, Pallas kernels, return_call(): pl.pallas_call(functools.partial(return_kernel, nz, ntp), out_shape=(jax....  25.4 us
    pallas_call x1, Pallas kernels, owner_call(): pl.pallas_call(functools.partial(owner_kernel, nz), out_shape=(jax.ShapeD...  11.9 us

profile of v7, /device:TPU:1, one launch (start us, length us, event | category | flops | bytes accessed | tf_op | source)
XLA Modules:
  0.0 70.0 jit_solution(1899079050485178945)
XLA Ops:
  0.6 31.4 %dispatch.1 = (bf16[8,2,8,16,128]{4,3,2,1,0:T(8,128)(2,1)S(1)}, s32[56,128]{1,0:T(8,128)S(1)}, f32[16,128]{1,0:T(8,128)S(1)}, f32[128,128]{1,0:T(8,128)S(1)}) custom-call(bf16[4,512]{1,0:T(4,128)(2,1)} %q_hbm.3, s32[4,128]{1,0:T(4,128)} %bitcast.2, s32[4,128]{1,0:T(4,128)} %bitcast.3, s32[4]{0:T(128)} %len_hbm.1), custom_call_target="tpu_custom_call" | custom-call | tf_op jit(solution)/shard_map/dispatch/pallas_call | solution.py:576
  32.0 0.0 copy-start
  32.0 11.9 %owner.1 = (bf16[8,16,16,128]{3,2,1,0:T(8,128)(2,1)S(1)}, f32[8,8,128]{2,1,0:T(8,128)S(1)}) custom-call(bf16[8,2,8,16,128]{4,3,2,1,0:T(8,128)(2,1)S(1)} %get-tuple-element.10.qall_ref, s32[56,128]{1,0:T(8,128)S(1)} %get-tuple-element.11.lists_ref, f32[16,128]{1,0:T(8,128)S(1)} %get-tuple-element.12.items_ref, f32[128,128]{1,0:T(8,128)S(1)} %get-tuple-element.13.sg_s, ...), custom_call_target="tpu_custom_call" | custom-call | tf_op jit(solution)/shard_map/owner/pallas_call | solution.py:552
  44.0 25.4 %give_back.1 = (f32[4,2048]{1,0:T(4,128)S(1)}, f32[4,2048]{1,0:T(4,128)S(1)}) custom-call(bf16[8,16,16,128]{3,2,1,0:T(8,128)(2,1)S(1)} %get-tuple-element.14.po_ref, f32[8,8,128]{2,1,0:T(8,128)S(1)} %get-tuple-element.15.ps_ref, bf16[4,512]{1,0:T(4,128)(2,1)} %q_hbm.3, bf16[4,128]{1,0:T(4,128)(2,1)} %fresh_hbm.1, bf16[512,2048]{1,0:T(8,128)(2,1)} %w_hbm.1, ...), custom_call_target="tpu_custom_call" | custom-call | tf_op jit(solution)/shard_map/give_back/pallas_call | solution.py:603
  69.3 0.0 copy-done
  69.4 0.6 multiply_convert_fusion
  (1 shorter events, 0.0 us)
Async XLA Ops:
  32.0 37.3 %copy-start = (bf16[2048]{0:T(1024)(128)(2,1)S(1)}, bf16[2048]{0:T(1024)(128)(2,1)}, u32[]{:S(2)}) copy-start(bf16[2048]{0:T(1024)(128)(2,1)} %param.17) | copy-start | bytes 12292

commit v8 on v7

--- a/solution.py
+++ b/solution.py
@@ -333,7 +333,7 @@
     want = jnp.where(same, ar // 4 % 4, -1).astype(F32)
     left16 = iota((16, 128), 1) < 64
 
-    @pl.loop(0, PLANE)
+    @pl.loop(0, PLANE, unroll=2)
     def _(d):
         for j in range(nz // 2):
             i = d * nz + 2 * j

time: 70.5 us -> 69.7 us (0.989)
  Pallas kernels: 68.7 us -> 67.5 us
    pallas_call x1, Pallas kernels: 11.9 us -> 10.6 us  [owner_call(): pl.pallas_call(functools.partial(owner_kernel, nz), out_shape=(jax.ShapeD...]
where the time goes in v8:
time: 69.7 us; the launch traced here: 68.8 us
  Pallas kernels  67.5 us (97%)
    pallas_call x1, Pallas kernels, dispatch_call(): pl.pallas_call(functools.partial(dispatch_kernel, nz, npages), out_shape=...  31.4 us
    pallas_call x1, Pallas kernels, return_call(): pl.pallas_call(functools.partial(return_kernel, nz, ntp), out_shape=(jax....  25.5 us
    pallas_call x1, Pallas kernels, owner_call(): pl.pallas_call(functools.partial(owner_kernel, nz), out_shape=(jax.ShapeD...  10.6 us

profile of v8, /device:TPU:1, one launch (start us, length us, event | category | flops | bytes accessed | tf_op | source)
XLA Modules:
  0.0 68.8 jit_solution(17868072435168428190)
XLA Ops:
  0.6 31.4 %dispatch.1 = (bf16[8,2,8,16,128]{4,3,2,1,0:T(8,128)(2,1)S(1)}, s32[56,128]{1,0:T(8,128)S(1)}, f32[16,128]{1,0:T(8,128)S(1)}, f32[128,128]{1,0:T(8,128)S(1)}) custom-call(bf16[4,512]{1,0:T(4,128)(2,1)} %q_hbm.3, s32[4,128]{1,0:T(4,128)} %bitcast.2, s32[4,128]{1,0:T(4,128)} %bitcast.3, s32[4]{0:T(128)} %len_hbm.1), custom_call_target="tpu_custom_call" | custom-call | tf_op jit(solution)/shard_map/dispatch/pallas_call | solution.py:576
  32.0 0.0 copy-start
  32.0 10.6 %owner.1 = (bf16[8,16,16,128]{3,2,1,0:T(8,128)(2,1)S(1)}, f32[8,8,128]{2,1,0:T(8,128)S(1)}) custom-call(bf16[8,2,8,16,128]{4,3,2,1,0:T(8,128)(2,1)S(1)} %get-tuple-element.10.qall_ref, s32[56,128]{1,0:T(8,128)S(1)} %get-tuple-element.11.lists_ref, f32[16,128]{1,0:T(8,128)S(1)} %get-tuple-element.12.items_ref, f32[128,128]{1,0:T(8,128)S(1)} %get-tuple-element.13.sg_s, ...), custom_call_target="tpu_custom_call" | custom-call | tf_op jit(solution)/shard_map/owner/pallas_call | solution.py:552
  42.7 25.5 %give_back.1 = (f32[4,2048]{1,0:T(4,128)S(1)}, f32[4,2048]{1,0:T(4,128)S(1)}) custom-call(bf16[8,16,16,128]{3,2,1,0:T(8,128)(2,1)S(1)} %get-tuple-element.14.po_ref, f32[8,8,128]{2,1,0:T(8,128)S(1)} %get-tuple-element.15.ps_ref, bf16[4,512]{1,0:T(4,128)(2,1)} %q_hbm.3, bf16[4,128]{1,0:T(4,128)(2,1)} %fresh_hbm.1, bf16[512,2048]{1,0:T(8,128)(2,1)} %w_hbm.1, ...), custom_call_target="tpu_custom_call" | custom-call | tf_op jit(solution)/shard_map/give_back/pallas_call | solution.py:603
  68.1 0.0 copy-done
  68.2 0.6 multiply_convert_fusion
  (1 shorter events, 0.0 us)
Async XLA Ops:
  32.0 36.1 %copy-start = (bf16[2048]{0:T(1024)(128)(2,1)S(1)}, bf16[2048]{0:T(1024)(128)(2,1)}, u32[]{:S(2)}) copy-start(bf16[2048]{0:T(1024)(128)(2,1)} %param.17) | copy-start | bytes 12292
